TPU v7x, 32 devices: a whole 2x2x4 slice. The times are simulated.
32 devices in a mesh: dp: 8 (over z, y), mp: 4 (over x, core).
Axes of the slice: x: 2, y: 2, z: 4, core: 2. Of those that a mesh axis runs over, the one named last changes fastest.
Arguments:
- hidden_in: bfloat16 [16384, 768], P('dp'), may hold values from -6 to 6
- cotangent: bfloat16 [16384, 768], P('dp'), may hold values from -6 to 6
- w_query: bfloat16 [768, 768], P('dp', 'mp'), may hold values from -0.3125 to 0.3125
- w_key: bfloat16 [768, 768], P('dp', 'mp'), may hold values from -0.21875 to 0.21875
- w_value: bfloat16 [768, 768], P('dp', 'mp'), may hold values from -0.21875 to 0.21875
- w_output: bfloat16 [768, 768], P('mp', 'dp'), may hold values from -0.4375 to 0.4375
- w_inner: bfloat16 [768, 3072], P('dp', 'mp'), may hold values from -0.21875 to 0.21875
- w_outer: bfloat16 [3072, 768], P('mp', 'dp'), may hold values from -0.109375 to 0.109375
- biases: bfloat16 [4, 768], P(None, 'dp'), may hold values from -3 to 3
- gains: bfloat16 [2, 768], P(None, 'dp'), may hold values from 0.5 to 1.5
- shifts: bfloat16 [2, 768], P(None, 'dp'), may hold values from -2 to 2
- inner_bias: bfloat16 [3072], P('dp'), may hold values from -3 to 3
- lengths: int32 [10], replicated, may hold values from 1024 to 2048, as said below
- padding: int32 [16384], P('dp'), may hold values from 0 to 1, as said below
- cluster_perm: int32 [12, 16384], P('mp', 'dp'), may hold values from 0 to 16383, as said below
Outputs:
- hidden_out: bfloat16 [16384, 768], P('dp')
- grad_hidden: bfloat16 [16384, 768], P('dp')
- grad_query: float32 [768, 768], P('dp', 'mp')
- grad_key: float32 [768, 768], P('dp', 'mp')
- grad_value: float32 [768, 768], P('dp', 'mp')
- grad_output: float32 [768, 768], P('mp', 'dp')
- grad_inner: float32 [768, 3072], P('dp', 'mp')
- grad_outer: float32 [3072, 768], P('mp', 'dp')
- grad_biases: float32 [4, 768], P(None, 'dp')
- grad_gains: float32 [2, 768], P(None, 'dp')
- grad_shifts: float32 [2, 768], P(None, 'dp')
- grad_inner_bias: float32 [3072], P('dp')
Inputs may be any that keep to these rules, and one draw needn't show every extreme that they name: In each run of 8 indices of dp, 10 lengths that, each rounded up to a multiple of 128, sum to 16384; in each run one of them is exactly 2048. `padding`: A row that is the p-th of its document's rows on its device, on index d of dp, is 1 exactly when p * 8 + (d mod 8) is under the document's length. `cluster_perm`: for each head a permutation of the token numbers; each cluster holds tokens of one document only, 16 from each device of its run; of the tokens held by one index of dp, exactly 256 have slots among those of each index r of dp (slots r * 2048 to (r + 1) * 2048 - 1).
All inputs are finite; a program needn't handle non-finite values.
Results may differ from a plain program's by a relative error of at most 0.015.
Values may be sent and summed in bfloat16 or wider, within the bound.
No kernel may reach another device: no remote copies, remote signals or barrier semaphores. Data moves between devices by JAX's collectives and lax.ppermute only.
A program may use at most 128 MiB of HBM per device.

v0:
```python
from functools import partial
import math

import jax
import jax.numpy as jnp
from jax import lax
from jax.sharding import PartitionSpec as P

D = 768
HEAD_DIM = 64
FF = 3072
CLUSTER = 128


epsilon = 1e-05
masked_fill = -1e30


def norm_forward(hidden, gain_row, shift_row):
    average = jnp.mean(hidden, axis=-1, keepdims=True)
    centred = hidden - average
    inv_std = lax.rsqrt(jnp.mean(centred * centred, axis=-1, keepdims=True) + epsilon)
    normed = centred * inv_std
    return (normed * gain_row + shift_row, normed, inv_std)


def norm_backward(upstream, normed, inv_std, gain_row):
    grad_gain = jnp.sum(upstream * normed, axis=0)
    grad_shift = jnp.sum(upstream, axis=0)
    scaled = upstream * gain_row
    centre_term = jnp.mean(scaled, axis=-1, keepdims=True)
    normal_term = normed * jnp.mean(scaled * normed, axis=-1, keepdims=True)
    return (inv_std * (scaled - centre_term - normal_term), grad_gain, grad_shift)


def cluster_view(row_data):
    return row_data.reshape((-1, CLUSTER) + row_data.shape[2:])


def pick_rows(row_data, row_index):
    return jnp.take_along_axis(row_data, row_index[:, :, None], axis=1)


def allowed_pairs(doc_slot, valid_slot):
    doc_blocks = cluster_view(doc_slot)
    valid_blocks = cluster_view(valid_slot)
    same_doc = doc_blocks[:, :, None] == doc_blocks[:, None, :]
    live_key = (valid_blocks == 1)[:, None, :]
    diagonal = jnp.eye(CLUSTER, dtype=bool)[None]
    return same_doc & live_key | diagonal


def masked_scores(queries, key_rows, permitted):
    score_scale = 1.0 / math.sqrt(queries.shape[-1])
    raw_scores = (
        jnp.einsum(
            "bid,bjd->bij",
            cluster_view(queries),
            cluster_view(key_rows),
            preferred_element_type=jnp.float32,
        )
        * score_scale
    )
    return jnp.where(permitted, raw_scores, masked_fill)


def attend(queries, key_rows, values, permitted):
    scores = masked_scores(queries, key_rows, permitted)
    row_max = jnp.max(scores, axis=-1, keepdims=True)
    denominator = jnp.sum(jnp.exp(scores - row_max), axis=-1, keepdims=True)
    logsum = row_max + jnp.log(denominator)
    soft_weights = jnp.exp(scores - logsum).astype(jnp.bfloat16)
    mixed_rows = jnp.einsum(
        "bij,bjd->bid", soft_weights, cluster_view(values), preferred_element_type=jnp.float32
    )
    return (mixed_rows.astype(jnp.bfloat16).reshape(queries.shape), logsum)


def attend_backward(queries, key_rows, values, permitted, logsum, grad_mixed):
    score_scale = 1.0 / math.sqrt(queries.shape[-1])
    soft_weights = jnp.exp(masked_scores(queries, key_rows, permitted) - logsum)
    grad_blocks = cluster_view(grad_mixed)
    grad_soft = jnp.einsum(
        "bid,bjd->bij", grad_blocks, cluster_view(values), preferred_element_type=jnp.float32
    )
    grad_values = jnp.einsum(
        "bij,bid->bjd",
        soft_weights.astype(jnp.bfloat16),
        grad_blocks,
        preferred_element_type=jnp.float32,
    )
    row_delta = jnp.sum(soft_weights * grad_soft, axis=-1, keepdims=True)
    grad_scores = (soft_weights * (grad_soft - row_delta)).astype(jnp.bfloat16)
    grad_queries = (
        jnp.einsum(
            "bij,bjd->bid", grad_scores, cluster_view(key_rows), preferred_element_type=jnp.float32
        )
        * score_scale
    )
    grad_keys = (
        jnp.einsum(
            "bij,bid->bjd", grad_scores, cluster_view(queries), preferred_element_type=jnp.float32
        )
        * score_scale
    )
    row_shape = queries.shape
    joined = jnp.concatenate(
        [
            grad_queries.reshape(row_shape),
            grad_keys.reshape(row_shape),
            grad_values.reshape(row_shape),
        ],
        axis=-1,
    )
    return joined.astype(jnp.bfloat16)


def on_device(
    hidden_in,
    cotangent,
    w_query,
    w_key,
    w_value,
    w_output,
    w_inner,
    w_outer,
    biases,
    gains,
    shifts,
    inner_bias,
    lengths,
    padding,
    cluster_perm,
):
    peer_count = lax.axis_size("dp")
    tokens = hidden_in.shape[0]
    heads_here = cluster_perm.shape[0]
    head_width = heads_here * HEAD_DIM
    ff_here = w_inner.shape[1]
    shard_index = lax.axis_index("mp")
    row_block = lax.axis_index("dp")
    stripe = min(16, peer_count)
    run_docs = lengths.shape[0] * stripe // peer_count
    run_index = row_block // stripe
    own_lengths = lax.dynamic_slice_in_dim(lengths, run_index * run_docs, run_docs, 0)
    local_rows = (own_lengths + CLUSTER - 1) // CLUSTER * CLUSTER // stripe
    local_ends = jnp.cumsum(local_rows)
    row_place = jnp.arange(tokens, dtype=jnp.int32)
    document = run_index * run_docs + jnp.sum(
        (row_place[:, None] >= local_ends[None, :]).astype(jnp.int32), axis=1
    )
    target = cluster_perm // tokens
    sorting = jnp.argsort(target, axis=1, stable=True)
    unsorting = jnp.argsort(sorting, axis=1)
    local_slot = jnp.take_along_axis(cluster_perm % tokens, sorting, axis=1)
    row_tags = jnp.stack(
        [local_slot, jnp.take(document, sorting), jnp.take(padding, sorting)], axis=-1
    )
    row_tags = row_tags.reshape(heads_here, peer_count, -1, 3)

    def to_peers(row_data, row_index):
        return pick_rows(row_data, row_index).reshape(
            (heads_here, peer_count, -1) + row_data.shape[2:]
        )

    def forward():
        gathered = (
            lax.all_gather(w_query, "dp", axis=0, tiled=True),
            lax.all_gather(w_key, "dp", axis=0, tiled=True),
            lax.all_gather(w_value, "dp", axis=0, tiled=True),
            lax.all_gather(w_inner, "dp", axis=0, tiled=True),
            lax.all_gather(w_output, "dp", axis=1, tiled=True),
            lax.all_gather(w_outer, "dp", axis=1, tiled=True),
            lax.all_gather(biases, "dp", axis=1, tiled=True),
            lax.all_gather(gains, "dp", axis=1, tiled=True),
            lax.all_gather(shifts, "dp", axis=1, tiled=True),
            lax.all_gather(inner_bias, "dp", axis=0, tiled=True),
        )
        (
            query_w,
            key_w,
            value_w,
            inner_w,
            output_w,
            outer_w,
            bias_all,
            gain_all,
            shift_all,
            inner_bias_all,
        ) = gathered
        bias_float = bias_all.astype(jnp.float32)
        gain_float = gain_all.astype(jnp.float32)
        shift_float = shift_all.astype(jnp.float32)

        def own_columns(vector):
            return lax.dynamic_slice_in_dim(vector, shard_index * head_width, head_width)

        queries = jnp.dot(hidden_in, query_w, preferred_element_type=jnp.float32) + own_columns(
            bias_float[0]
        )
        key_rows = jnp.dot(hidden_in, key_w, preferred_element_type=jnp.float32)
        values = jnp.dot(hidden_in, value_w, preferred_element_type=jnp.float32) + own_columns(
            bias_float[1]
        )
        packed = jnp.concatenate(
            [
                matrix.reshape(tokens, heads_here, HEAD_DIM)
                for matrix in (queries, key_rows, values)
            ],
            axis=2,
        )
        packed = packed.astype(jnp.bfloat16).transpose(1, 0, 2)
        arrived, arrived_tags = (
            lax.all_to_all(
                to_peers(packed, sorting), "dp", split_axis=1, concat_axis=1, tiled=True
            ),
            lax.all_to_all(row_tags, "dp", split_axis=1, concat_axis=1, tiled=True),
        )
        arrived = arrived.reshape(heads_here, tokens, 3 * HEAD_DIM)
        arrived_tags = arrived_tags.reshape(heads_here, tokens, 3)
        arrival_slot = arrived_tags[:, :, 0]
        slot_arrival = jnp.argsort(arrival_slot, axis=1)
        in_slots = pick_rows(arrived, slot_arrival)
        slot_tags = pick_rows(arrived_tags, slot_arrival)
        permitted = allowed_pairs(slot_tags[:, :, 1], slot_tags[:, :, 2])
        slot_query = in_slots[:, :, :HEAD_DIM]
        slot_key = in_slots[:, :, HEAD_DIM : 2 * HEAD_DIM]
        slot_value = in_slots[:, :, 2 * HEAD_DIM :]
        mixed_rows, logsum = attend(slot_query, slot_key, slot_value, permitted)
        returned = lax.all_to_all(
            to_peers(mixed_rows, arrival_slot), "dp", split_axis=1, concat_axis=1, tiled=True
        )
        attended = pick_rows(returned.reshape(heads_here, tokens, HEAD_DIM), unsorting)
        attended = attended.transpose(1, 0, 2).reshape(tokens, head_width)
        attn_terms = jnp.dot(attended, output_w, preferred_element_type=jnp.float32)
        branch = lax.psum(attn_terms, "mp") + bias_float[2]
        residual_in = hidden_in.astype(jnp.float32)
        first, normed_one, inv_one = norm_forward(
            residual_in + branch, gain_float[0], shift_float[0]
        )
        first_low = first.astype(jnp.bfloat16)
        own_inner_bias = lax.dynamic_slice_in_dim(
            inner_bias_all, shard_index * ff_here, ff_here
        ).astype(jnp.float32)
        pre_act = jnp.dot(first_low, inner_w, preferred_element_type=jnp.float32) + own_inner_bias
        activated = jax.nn.gelu(pre_act, approximate=False).astype(jnp.bfloat16)
        ffn_terms = jnp.dot(activated, outer_w, preferred_element_type=jnp.float32)
        ffn_out = lax.psum(ffn_terms, "mp") + bias_float[3]
        result, normed_two, inv_two = norm_forward(first + ffn_out, gain_float[1], shift_float[1])
        result_low = result.astype(jnp.bfloat16)
        return {
            "query_w": query_w,
            "key_w": key_w,
            "value_w": value_w,
            "inner_w": inner_w,
            "output_w": output_w,
            "outer_w": outer_w,
            "gain_float": gain_float,
            "arrival_slot": arrival_slot,
            "slot_arrival": slot_arrival,
            "permitted": permitted,
            "slot_query": slot_query,
            "slot_key": slot_key,
            "slot_value": slot_value,
            "logsum": logsum,
            "attended": attended,
            "normed_one": normed_one,
            "inv_one": inv_one,
            "first_low": first_low,
            "pre_act": pre_act,
            "activated": activated,
            "normed_two": normed_two,
            "inv_two": inv_two,
            "result": result_low,
        }

    first_pass = forward()
    kept = forward()
    hidden_out = first_pass["result"]
    upstream = cotangent.astype(jnp.float32)
    grad_h2, grad_gain_two, grad_shift_two = norm_backward(
        upstream, kept["normed_two"], kept["inv_two"], kept["gain_float"][1]
    )
    grad_ffn = grad_h2.astype(jnp.bfloat16)
    grad_outer_w = jnp.einsum(
        "tf,td->fd", kept["activated"], grad_ffn, preferred_element_type=jnp.float32
    )
    grad_act = jnp.einsum(
        "td,fd->tf", grad_ffn, kept["outer_w"], preferred_element_type=jnp.float32
    )
    _, gelu_pull = jax.vjp(partial(jax.nn.gelu, approximate=False), kept["pre_act"])
    grad_pre = gelu_pull(grad_act)[0].astype(jnp.bfloat16)
    grad_inner_w = jnp.einsum(
        "td,tf->df", kept["first_low"], grad_pre, preferred_element_type=jnp.float32
    )
    inner_bias_part = jnp.sum(grad_pre.astype(jnp.float32), axis=0)
    inner_bias_full = lax.dynamic_update_slice_in_dim(
        jnp.zeros((FF,), jnp.float32), inner_bias_part, shard_index * ff_here, 0
    )
    first_part = jnp.einsum(
        "tf,df->td", grad_pre, kept["inner_w"], preferred_element_type=jnp.float32
    )
    first_sum, inner_bias_grad = lax.psum((first_part, inner_bias_full), "mp")
    grad_first = grad_h2 + first_sum
    grad_h1, grad_gain_one, grad_shift_one = norm_backward(
        grad_first, kept["normed_one"], kept["inv_one"], kept["gain_float"][0]
    )
    grad_branch = grad_h1.astype(jnp.bfloat16)
    grad_output_w = jnp.einsum(
        "te,td->ed", kept["attended"], grad_branch, preferred_element_type=jnp.float32
    )
    grad_attended = jnp.einsum(
        "td,ed->te", grad_branch, kept["output_w"], preferred_element_type=jnp.float32
    ).astype(jnp.bfloat16)
    grad_rows = grad_attended.reshape(tokens, heads_here, HEAD_DIM).transpose(1, 0, 2)
    grad_arrived = lax.all_to_all(
        to_peers(grad_rows, sorting), "dp", split_axis=1, concat_axis=1, tiled=True
    )
    grad_slots = pick_rows(grad_arrived.reshape(heads_here, tokens, HEAD_DIM), kept["slot_arrival"])
    slot_grads = attend_backward(
        kept["slot_query"],
        kept["slot_key"],
        kept["slot_value"],
        kept["permitted"],
        kept["logsum"],
        grad_slots,
    )
    grad_returned = lax.all_to_all(
        to_peers(slot_grads, kept["arrival_slot"]), "dp", split_axis=1, concat_axis=1, tiled=True
    )
    token_grads = pick_rows(
        grad_returned.reshape(heads_here, tokens, 3 * HEAD_DIM), unsorting
    ).transpose(1, 0, 2)
    grad_queries = token_grads[:, :, :HEAD_DIM].reshape(tokens, head_width)
    grad_keys = token_grads[:, :, HEAD_DIM : 2 * HEAD_DIM].reshape(tokens, head_width)
    grad_values = token_grads[:, :, 2 * HEAD_DIM :].reshape(tokens, head_width)
    grad_query_w = jnp.einsum(
        "td,te->de", hidden_in, grad_queries, preferred_element_type=jnp.float32
    )
    grad_key_w = jnp.einsum("td,te->de", hidden_in, grad_keys, preferred_element_type=jnp.float32)
    grad_value_w = jnp.einsum(
        "td,te->de", hidden_in, grad_values, preferred_element_type=jnp.float32
    )
    hidden_part = jnp.einsum(
        "te,de->td", grad_queries, kept["query_w"], preferred_element_type=jnp.float32
    )
    hidden_part = hidden_part + jnp.einsum(
        "te,de->td", grad_keys, kept["key_w"], preferred_element_type=jnp.float32
    )
    hidden_part = hidden_part + jnp.einsum(
        "te,de->td", grad_values, kept["value_w"], preferred_element_type=jnp.float32
    )
    head_bias_part = jnp.stack(
        [
            jnp.sum(grad_queries.astype(jnp.float32), axis=0),
            jnp.sum(grad_values.astype(jnp.float32), axis=0),
        ]
    )
    head_bias_full = lax.dynamic_update_slice_in_dim(
        jnp.zeros((2, D), jnp.float32), head_bias_part, shard_index * head_width, 1
    )
    gain_grads = jnp.stack([grad_gain_one, grad_gain_two])
    shift_grads = jnp.stack([grad_shift_one, grad_shift_two])
    hidden_sum, head_bias_grad = (
        lax.psum(hidden_part.astype(jnp.bfloat16), "mp").astype(jnp.float32),
        lax.psum(head_bias_full.astype(jnp.bfloat16), "mp").astype(jnp.float32),
    )
    grad_hidden = (grad_h1 + hidden_sum).astype(jnp.bfloat16)
    bias_grads = jnp.stack(
        [
            head_bias_grad[0],
            head_bias_grad[1],
            jnp.sum(grad_branch.astype(jnp.float32), axis=0),
            jnp.sum(grad_ffn.astype(jnp.float32), axis=0),
        ]
    )
    reduced = (
        lax.psum_scatter(grad_query_w, "dp", scatter_dimension=0, tiled=True),
        lax.psum_scatter(grad_key_w, "dp", scatter_dimension=0, tiled=True),
        lax.psum_scatter(grad_value_w, "dp", scatter_dimension=0, tiled=True),
        lax.psum_scatter(grad_inner_w, "dp", scatter_dimension=0, tiled=True),
        lax.psum_scatter(grad_output_w, "dp", scatter_dimension=1, tiled=True),
        lax.psum_scatter(grad_outer_w, "dp", scatter_dimension=1, tiled=True),
        lax.psum_scatter(bias_grads, "dp", scatter_dimension=1, tiled=True),
        lax.psum_scatter(gain_grads, "dp", scatter_dimension=1, tiled=True),
        lax.psum_scatter(shift_grads, "dp", scatter_dimension=1, tiled=True),
        lax.psum_scatter(inner_bias_grad, "dp", scatter_dimension=0, tiled=True),
    )
    return (
        hidden_out,
        grad_hidden,
        reduced[0],
        reduced[1],
        reduced[2],
        reduced[4],
        reduced[3],
        reduced[5],
        reduced[6],
        reduced[7],
        reduced[8],
        reduced[9],
    )


def solution(mesh):
    placed = (
        P("dp", None),
        P("dp", None),
        P("dp", "mp"),
        P("dp", "mp"),
        P("dp", "mp"),
        P("mp", "dp"),
        P("dp", "mp"),
        P("mp", "dp"),
        P(None, "dp"),
        P(None, "dp"),
        P(None, "dp"),
        P("dp"),
        P(),
        P("dp"),
        P("mp", "dp"),
    )
    return jax.shard_map(
        on_device,
        mesh=mesh,
        in_specs=placed,
        out_specs=(
            P("dp", None),
            P("dp", None),
            P("dp", "mp"),
            P("dp", "mp"),
            P("dp", "mp"),
            P("mp", "dp"),
            P("dp", "mp"),
            P("mp", "dp"),
            P(None, "dp"),
            P(None, "dp"),
            P(None, "dp"),
            P("dp"),
        ),
        check_vma=False,
    )
```

profile of v0, /device:TPU:0, one launch (start us, length us, event | category | flops | bytes accessed | tf_op | source)
XLA Modules:
  0.0 1926.6 jit_solution(14494883081744845638)
XLA Ops:
  11.1 22.5 %all-gather = bf16[8,96,4]{1,2,0:T(4,128)(2,1)S(1)} all-gather(bf16[1,96,4]{1,2,0:T(4,128)(2,1)} %bitcast.229), channel_id=1, replica_groups=mesh['dp'=8,'mp'=4] {'dp'}, dimensions={0}, use_global_device_ids=true | all-gather | bytes 6912 | tf_op jit(solution)/shard_map/all_gather | solution.py:174
  34.3 33.3 %all_gather.40 = bf16[768,192]{1,0:T(8,128)(2,1)} all-gather(bf16[96,192]{1,0:T(8,128)(2,1)} %param.25), channel_id=1, replica_groups=mesh['dp'=8,'mp'=4] {'dp'}, dimensions={0}, use_global_device_ids=true | all-gather | bytes 331776 | tf_op jit(solution)/shard_map/all_gather | solution.py:168
  74.4 31.1 %all_gather.43 = bf16[768,192]{1,0:T(8,128)(2,1)S(1)} all-gather(bf16[96,192]{1,0:T(8,128)(2,1)S(1)} %copy-done.40), channel_id=1, replica_groups=mesh['dp'=8,'mp'=4] {'dp'}, dimensions={0}, use_global_device_ids=true | all-gather | bytes 331776 | tf_op jit(solution)/shard_map/all_gather | solution.py:170
  110.8 30.9 %all_gather.42 = bf16[768,192]{1,0:T(8,128)(2,1)S(1)} all-gather(bf16[96,192]{1,0:T(8,128)(2,1)S(1)} %copy-done.41), channel_id=1, replica_groups=mesh['dp'=8,'mp'=4] {'dp'}, dimensions={0}, use_global_device_ids=true | all-gather | bytes 331776 | tf_op jit(solution)/shard_map/all_gather | solution.py:169
  151.8 52.1 %gather_fusion = s32[6144]{0:T(1024)S(1)} fusion(s32[3,2048]{1,0:T(4,128)S(1)} %get-tuple-element.135, s32[6144]{0:T(1024)S(1)} %reshape.362), kind=kCustom, calls=%fused_computation.11 | custom fusion | bytes 98304 | tf_op jit(solution)/shard_map/jit(take_along_axis)/gather | solution.py:155
  204.0 34.3 %gather_fusion.1 = s32[6144]{0:T(1024)S(1)} fusion(s32[2048]{0:T(1024)S(1)} %broadcast_add_fusion, s32[6144]{0:T(1024)S(1)} %broadcast_clamp_fusion), kind=kCustom, calls=%fused_computation.clone | custom fusion | bytes 73728 | tf_op jit(solution)/shard_map/jit(_take)/gather | solution.py:157
  238.3 34.3 %gather_fusion.2 = s32[6144]{0:T(1024)S(1)} fusion(s32[2048]{0:T(1024)S(1)} %copy-done, s32[6144]{0:T(1024)S(1)} %broadcast_clamp_fusion), kind=kCustom, calls=%fused_computation.4.clone | custom fusion | bytes 73728 | tf_op jit(solution)/shard_map/jit(_take)/gather | solution.py:157
  276.7 61.3 %gather_fusion.4 = bf16[6144,192]{1,0:T(8,128)(2,1)} fusion(bf16[3,2048,192]{2,1,0:T(8,128)(2,1)S(1)} %maximum_bitcast_fusion, s32[6144]{0:T(1024)S(1)} %reshape.400), kind=kCustom, calls=%fused_computation.2.clone | custom fusion | bytes 4767744 | tf_op jit(solution)/shard_map/jit(take_along_axis)/gather | solution.py:41
  361.9 66.9 %gather_fusion.3 = s32[6144,3]{1,0:T(8,128)} fusion(s32[3,2048,3]{2,1,0:T(8,128)S(1)} %bitcast.180, s32[6144]{0:T(1024)S(1)} %reshape.396), kind=kCustom, calls=%fused_computation.1.clone | custom fusion | bytes 196608 | tf_op jit(solution)/shard_map/jit(take_along_axis)/gather | solution.py:41
  434.7 61.3 %gather_fusion.5 = bf16[6144,192]{1,0:T(8,128)(2,1)} fusion(bf16[3,2048,192]{2,1,0:T(8,128)(2,1)S(1)} %bitcast.182, s32[6144]{0:T(1024)S(1)} %reshape.396), kind=kCustom, calls=%fused_computation.5.clone | custom fusion | bytes 4767744 | tf_op jit(solution)/shard_map/jit(take_along_axis)/gather | solution.py:41
  521.9 32.3 %gather_fusion.6 = bf16[6144,64]{1,0:T(8,128)(2,1)S(1)} fusion(bf16[3,2048,64]{2,1,0:T(8,128)(2,1)S(1)} %bitcast.185, s32[6144]{0:T(1024)S(1)} %reshape.408), kind=kCustom, calls=%fused_computation.3.clone | custom fusion | bytes 1622016 | tf_op jit(solution)/shard_map/jit(take_along_axis)/gather | solution.py:41
  562.9 38.4 %all_gather.44 = bf16[192,768]{0,1:T(8,128)(2,1)} all-gather(bf16[192,96]{0,1:T(8,128)(2,1)S(1)} %copy.248), channel_id=1, replica_groups=mesh['dp'=8,'mp'=4] {'dp'}, dimensions={1}, use_global_device_ids=true | all-gather | bytes 331776 | tf_op jit(solution)/shard_map/all_gather | solution.py:172
  603.9 32.3 %gather_fusion.7 = bf16[6144,64]{1,0:T(8,128)(2,1)S(1)} fusion(bf16[3,2048,64]{2,1,0:T(8,128)(2,1)S(1)} %bitcast.186, s32[6144]{0:T(1024)S(1)} %reshape.412), kind=kCustom, calls=%fused_computation.8.clone | custom fusion | bytes 1622016 | tf_op jit(solution)/shard_map/jit(take_along_axis)/gather | solution.py:41
  659.3 18.0 all-gather.2
  677.4 25.9 %all-gather.3 = bf16[8,1,384]{2,1,0:T(2,128)(2,1)S(1)} all-gather(bf16[1,1,384]{2,1,0:T(2,128)(2,1)S(1)} %reshape.383), channel_id=1, replica_groups=mesh['dp'=8,'mp'=4] {'dp'}, dimensions={0}, use_global_device_ids=true | all-gather | bytes 6912 | tf_op jit(solution)/shard_map/all_gather | solution.py:177
  703.5 55.0 %all-reduce.6.cloned.1.call-done = f32[2048,768]{1,0:T(8,128)} async-done(((f32[2048,768]{1,0:T(8,128)}), f32[2048,768]{1,0:T(8,128)}) %all-reduce.6.cloned.1.call-update) | async-done | bytes 6291472 | tf_op jit(solution)/shard_map/psum | solution.py:236
  766.1 19.8 %multiply_convert_fusion = (bf16[2048,768]{1,0:T(8,128)(2,1)}, f32[2048,768]{1,0:T(8,128)}, f32[2048,768]{1,0:T(8,128)}) fusion(f32[768]{0:T(1024)S(1)} %dynamic-slice_convert_fusion, bf16[2048,768]{1,0:T(8,128)(2,1)S(1)} %fusion.13, bf16[768,768]{1,0:T(8,128)(2,1)} %all-gather.7.cloned.1.call-done), kind=kOutput, calls=%fused_computation.37 | convolution fusion | flops 2519728128 | bytes 20057088 | tf_op jit(solution)/shard_map/dot_general | solution.py:245
  793.5 119.9 %all-reduce.8.cloned.1.call-done = f32[2048,768]{1,0:T(8,128)} async-done(((f32[2048,768]{1,0:T(8,128)}), f32[2048,768]{1,0:T(8,128)}) %all-reduce.8.cloned.1.call-update) | async-done | bytes 6291472 | tf_op jit(solution)/shard_map/psum | solution.py:248
  944.0 119.9 %all-reduce.10.cloned.1.call-done = f32[2048,768]{1,0:T(8,128)} async-done(((f32[2048,768]{1,0:T(8,128)}), f32[2048,768]{1,0:T(8,128)}) %all-reduce.10.cloned.1.call-update) | async-done | bytes 6291472 | tf_op jit(solution)/shard_map/psum | solution.py:303
  1080.3 32.3 %gather_fusion.8 = bf16[6144,64]{1,0:T(8,128)(2,1)S(1)} fusion(bf16[3,2048,64]{2,1,0:T(8,128)(2,1)S(1)} %bitcast.183, s32[6144]{0:T(1024)S(1)} %copy-done.3), kind=kCustom, calls=%fused_computation.9.clone | custom fusion | bytes 1622016 | tf_op jit(solution)/shard_map/jit(take_along_axis)/gather | solution.py:41
  1113.5 25.4 %all_to_all.28 = bf16[3,8,256,64]{2,3,0,1:T(8,128)(2,1)S(1)} all-to-all(bf16[3,8,256,64]{2,3,0,1:T(8,128)(2,1)S(1)} %bitcast.212), channel_id=1, replica_groups=mesh['dp'=8,'mp'=4] {'dp'}, dimensions={1} | all-to-all | bytes 1572864 | tf_op jit(solution)/shard_map/all_to_all | solution.py:316
  1139.8 60.0 %gather_fusion.9 = bf16[6144,64]{1,0:T(8,128)(2,1)} fusion(bf16[3,2048,64]{2,1,0:T(8,128)(2,1)S(1)} %bitcast.184, s32[6144]{0:T(1024)S(1)} %reshape.396), kind=kCustom, calls=%fused_computation.10.clone | custom fusion | bytes 1622016 | tf_op jit(solution)/shard_map/jit(take_along_axis)/gather | solution.py:41
  1229.1 60.8 %gather_fusion.10 = bf16[6144,192]{1,0:T(8,128)(2,1)} fusion(bf16[3,2048,192]{2,1,0:T(8,128)(2,1)S(1)} %pad_maximum_fusion, s32[6144]{0:T(1024)S(1)} %reshape.408), kind=kCustom, calls=%fused_computation.6.clone | custom fusion | bytes 4767744 | tf_op jit(solution)/shard_map/jit(take_along_axis)/gather | solution.py:41
  1307.3 48.5 %all-to-all-done.4 = bf16[3,8,256,192]{2,3,0,1:T(8,128)(2,1)} async-done(((bf16[3,8,256,192]{2,3,0,1:T(8,128)(2,1)}), bf16[3,8,256,192]{2,3,0,1:T(8,128)(2,1)}, u32[]{:S(2)}, u32[]{:S(2)}) %all-to-all-start.4) | async-done | bytes 2359328 | tf_op jit(solution)/shard_map/all_to_all | solution.py:328
  1358.8 60.8 %gather_fusion.11 = bf16[6144,192]{1,0:T(8,128)(2,1)} fusion(bf16[3,2048,192]{2,1,0:T(8,128)(2,1)S(1)} %bitcast.181, s32[6144]{0:T(1024)S(1)} %copy-done.5), kind=kCustom, calls=%fused_computation.7.clone | custom fusion | bytes 4767744 | tf_op jit(solution)/shard_map/jit(take_along_axis)/gather | solution.py:41
  1481.8 35.9 %all-reduce = f32[3072]{0:T(1024)S(1)} all-reduce(f32[3072]{0:T(1024)S(1)} %dynamic_update_slice.7), channel_id=11, replica_groups=mesh['dp'=8,'mp'=4] {'dp'}, use_global_device_ids=true, to_apply=%region_40.45.clone | all-reduce | flops 3072 | bytes 24576
  1528.6 48.6 %reduce-scatter.36.cloned.1.call-done = f32[96,4]{1,0:T(8,128)} async-done(((f32[768,4]{1,0:T(8,128)}), f32[96,4]{1,0:T(8,128)}) %reduce-scatter.36.cloned.1.call-update) | async-done | bytes 1552
  1584.7 64.7 %reduce-scatter.26.cloned.1.call-done = f32[768,96]{0,1:T(8,128)} async-done(((f32[768,768]{0,1:T(8,128)}), f32[768,96]{0,1:T(8,128)}) %reduce-scatter.26.cloned.1.call-update) | async-done | bytes 294928 | tf_op jit(solution)/shard_map/reduce_scatter | solution.py:383
  1649.5 72.4 %reduce-scatter.24.cloned.1.call-done = f32[96,768]{1,0:T(8,128)} async-done(((f32[768,768]{1,0:T(8,128)}), f32[96,768]{1,0:T(8,128)}) %reduce-scatter.24.cloned.1.call-update) | async-done | bytes 294928 | tf_op jit(solution)/shard_map/reduce_scatter | solution.py:381
  1721.9 65.7 %reduce-scatter.28.cloned.1.call-done = f32[96,192]{1,0:T(8,128)} async-done(((f32[768,192]{1,0:T(8,128)}), f32[96,192]{1,0:T(8,128)}) %reduce-scatter.28.cloned.1.call-update) | async-done | bytes 73744
  1787.6 65.5 %reduce-scatter.30.cloned.1.call-done = f32[96,192]{1,0:T(8,128)} async-done(((f32[768,192]{1,0:T(8,128)}), f32[96,192]{1,0:T(8,128)}) %reduce-scatter.30.cloned.1.call-update) | async-done | bytes 73744
  1853.1 65.7 %reduce-scatter.32.cloned.1.call-done = f32[96,192]{1,0:T(8,128)} async-done(((f32[768,192]{1,0:T(8,128)}), f32[96,192]{1,0:T(8,128)}) %reduce-scatter.32.cloned.1.call-update) | async-done | bytes 73744
  (332 shorter events, 312.6 us)
Async XLA Ops:
  8.0 230.3 %copy-start = (s32[2048]{0:T(1024)S(1)}, s32[2048]{0:T(1024)}, u32[]{:S(2)}) copy-start(s32[2048]{0:T(1024)} %param.36) | copy-start | bytes 24580
  8.0 142.1 %sort.50.cloned.1.call-start = ((), (), s32[]{:S(2)}) async-start(), calls=%async_computation.29 | async-start | bytes 196640 | tf_op jit(solution)/shard_map/jit(argsort)/sort | solution.py:153
  67.7 38.5 %copy-start.10 = (bf16[2048,768]{1,0:T(8,128)(2,1)S(1)}, bf16[2048,768]{1,0:T(8,128)(2,1)}, u32[]{:S(2)}) copy-start(bf16[2048,768]{1,0:T(8,128)(2,1)} %param.23) | copy-start | bytes 9437188
  151.7 189.5 %copy-start.36 = (pred[3,2048]{1,0:T(4,128)(4,1)}, pred[3,2048]{1,0:T(4,128)(4,1)S(1)}, u32[]{:S(2)}) copy-start(pred[3,2048]{1,0:T(4,128)(4,1)S(1)} %and_bitcast_fusion.1) | copy-start | bytes 18436
  151.8 52.2 %copy-start.32 = (s32[3,2048]{1,0:T(4,128)S(1)}, s32[3,2048]{1,0:T(4,128)}, u32[]{:S(2)}) copy-start(s32[3,2048]{1,0:T(4,128)} %get-tuple-element.19) | copy-start | bytes 73732
  273.3 69.9 %all-to-all-start = ((s32[3,8,256,3]{2,0,3,1:T(4,128)}), s32[3,8,256,3]{2,0,3,1:T(4,128)S(1)}, u32[]{:S(2)}, u32[]{:S(2)}) async-start(s32[3,8,256,3]{2,0,3,1:T(4,128)} %pad_add_fusion), calls=%async_computation | async-start | bytes 196608 | tf_op jit(solution)/shard_map/all_to_all | solution.py:217
  276.7 61.4 %copy-start.2 = (s32[6144]{0:T(1024)}, s32[6144]{0:T(1024)S(1)}, u32[]{:S(2)}) copy-start(s32[6144]{0:T(1024)S(1)} %reshape.400) | copy-start | bytes 73732
  343.2 88.5 %all-to-all-start.1 = ((bf16[3,8,256,192]{2,3,0,1:T(8,128)(2,1)}), bf16[3,8,256,192]{2,3,0,1:T(8,128)(2,1)}, u32[]{:S(2)}, u32[]{:S(2)}) async-start(bf16[3,8,256,192]{2,3,0,1:T(8,128)(2,1)} %bitcast.175), calls=%async_computation.1 | async-start | bytes 4718592 | tf_op jit(solution)/shard_map/all_to_all | solution.py:214
  354.8 200.1 %copy-start.34 = (pred[3,2048]{1,0:T(4,128)(4,1)}, pred[3,2048]{1,0:T(4,128)(4,1)S(1)}, u32[]{:S(2)}) copy-start(pred[3,2048]{1,0:T(4,128)(4,1)S(1)} %and_reduce_fusion) | copy-start | bytes 18436
  556.0 47.0 %all-to-all-start.2 = ((bf16[3,8,256,64]{2,3,0,1:T(8,128)(2,1)}), bf16[3,8,256,64]{2,3,0,1:T(8,128)(2,1)S(1)}, u32[]{:S(2)}, u32[]{:S(2)}) async-start(bf16[3,8,256,64]{2,3,0,1:T(8,128)(2,1)} %bitcast.177), calls=%async_computation.2 | async-start | bytes 1572864 | tf_op jit(solution)/shard_map/all_to_all | solution.py:230
  562.0 39.3 %sort.54.cloned.1.call-start = ((), (), s32[]{:S(2)}) async-start(), calls=%async_computation.31 | async-start | bytes 196640 | tf_op jit(solution)/shard_map/jit(argsort)/sort | solution.py:154
  562.9 195.6 %all-reduce.6.cloned.1.call-start = ((), (), s32[]{:S(2)}) async-start(), calls=%async_computation.14 | async-start | bytes 12582912 | tf_op jit(solution)/shard_map/psum | solution.py:236
  641.6 35.8 %copy-start.45 = (bf16[384]{0:T(512)(128)(2,1)S(1)}, bf16[384]{0:T(512)(128)(2,1)}, u32[]{:S(2)}) copy-start(bf16[384]{0:T(512)(128)(2,1)} %param.34) | copy-start | bytes 2308
  641.6 116.9 %copy-start.11 = (bf16[2048,768]{1,0:T(8,128)(2,1)S(1)}, bf16[2048,768]{1,0:T(8,128)(2,1)}, u32[]{:S(2)}) copy-start(bf16[2048,768]{1,0:T(8,128)(2,1)} %param.23) | copy-start | bytes 9437188
  641.6 124.5 %all-gather.7.cloned.1.call-start = ((), (), s32[]{:S(2)}) async-start(), calls=%async_computation.15 | async-start | bytes 1327104 | tf_op jit(solution)/shard_map/all_gather | solution.py:171
  642.2 143.7 %all-gather.9.cloned.1.call-start = ((), (), s32[]{:S(2)}) async-start(), calls=%async_computation.16 | async-start | bytes 1327104 | tf_op jit(solution)/shard_map/all_gather | solution.py:173
  642.8 270.6 %all-reduce.8.cloned.1.call-start = ((), (), s32[]{:S(2)}) async-start(), calls=%async_computation.17 | async-start | bytes 12582912 | tf_op jit(solution)/shard_map/psum | solution.py:248
  793.5 120.0 %copy-start.43 = (f32[768]{0:T(1024)S(1)}, f32[768]{0:T(1024)}, u32[]{:S(2)}) copy-start(f32[768]{0:T(1024)} %get-tuple-element.106) | copy-start | bytes 9220
  793.5 270.4 %all-reduce.10.cloned.1.call-start = ((), (), s32[]{:S(2)}) async-start(), calls=%async_computation.18 | async-start | bytes 12582912 | tf_op jit(solution)/shard_map/psum | solution.py:303
  1295.0 60.7 %all-to-all-start.4 = ((bf16[3,8,256,192]{2,3,0,1:T(8,128)(2,1)}), bf16[3,8,256,192]{2,3,0,1:T(8,128)(2,1)}, u32[]{:S(2)}, u32[]{:S(2)}) async-start(bf16[3,8,256,192]{2,3,0,1:T(8,128)(2,1)} %bitcast.174), calls=%async_computation.4 | async-start | bytes 4718592 | tf_op jit(solution)/shard_map/all_to_all | solution.py:328
  1299.6 224.5 %reduce-scatter.40.cloned.1.call-start = ((), (), s32[]{:S(2)}) async-start(), calls=%async_computation.28 | async-start | bytes 442368
  1300.6 224.9 %reduce-scatter.38.cloned.1.call-start = ((), (), s32[]{:S(2)}) async-start(), calls=%async_computation.27 | async-start | bytes 442368
  1301.7 225.2 %reduce-scatter.34.cloned.1.call-start = ((), (), s32[]{:S(2)}) async-start(), calls=%async_computation.25 | async-start | bytes 884736
  1307.2 51.6 %copy-start.5 = (s32[6144]{0:T(1024)S(1)}, s32[6144]{0:T(1024)}, u32[]{:S(2)}) copy-start(s32[6144]{0:T(1024)} %copy-done.4) | copy-start | bytes 73732
  1307.2 270.0 %reduce-scatter.36.cloned.1.call-start = ((), (), s32[]{:S(2)}) async-start(), calls=%async_computation.26 | async-start | bytes 442368
  1441.0 137.6 %all-reduce.12.cloned.1.call-start = ((), (), s32[]{:S(2)}) async-start(), calls=%async_computation.19 | async-start | bytes 6291456 | tf_op jit(solution)/shard_map/psum | solution.py:365
  1448.6 200.8 %reduce-scatter.26.cloned.1.call-start = ((), (), s32[]{:S(2)}) async-start(), calls=%async_computation.21 | async-start | bytes 2654208 | tf_op jit(solution)/shard_map/reduce_scatter | solution.py:383
  1457.5 264.3 %reduce-scatter.24.cloned.1.call-start = ((), (), s32[]{:S(2)}) async-start(), calls=%async_computation.20 | async-start | bytes 2654208 | tf_op jit(solution)/shard_map/reduce_scatter | solution.py:381
  1464.9 322.7 %reduce-scatter.28.cloned.1.call-start = ((), (), s32[]{:S(2)}) async-start(), calls=%async_computation.22 | async-start | bytes 884736
  1470.0 383.1 %reduce-scatter.30.cloned.1.call-start = ((), (), s32[]{:S(2)}) async-start(), calls=%async_computation.23 | async-start | bytes 884736
  1475.1 443.7 %reduce-scatter.32.cloned.1.call-start = ((), (), s32[]{:S(2)}) async-start(), calls=%async_computation.24 | async-start | bytes 884736
  1578.7 340.2 %copy-start.1 = (s32[2048]{0:T(1024)S(1)}, s32[2048]{0:T(1024)}, u32[]{:S(2)}) copy-start(s32[2048]{0:T(1024)} %param.36) | copy-start | bytes 24580
  (45 other events, 322.8 us)
Sparse Core Ops, SparseCore 0:
  11.9 3.3 sort.56.cloned.1.call-done
  353.9 6.9 sort.58.cloned.1.call-done
  565.9 6.3 sort.60.cloned.1.call-done
  641.7 116.7 all-reduce.5
  793.6 119.7 all-reduce.7
  944.1 119.7 all-reduce.9
  1448.8 67.6 all-reduce.11
  (3 shorter events, 0.0 us)
Sparse Core Ops, SparseCore 1:
  644.3 38.5 all-gather.6
  684.9 39.8 all-gather.8
  1303.3 80.9 reduce-scatter.39
  1387.5 60.5 reduce-scatter.37
  1451.4 61.6 reduce-scatter.33
  1516.7 60.5 reduce-scatter.35
  1581.5 67.9 reduce-scatter.25
  1653.8 68.0 reduce-scatter.23
  1726.0 61.6 reduce-scatter.27
  1791.5 61.5 reduce-scatter.29
  1857.2 61.6 reduce-scatter.31
where the time goes:
time: 1940 us; the launch traced here: 1930 us
  waiting for transfers between devices  727 us (37%)
  local copies, waits for them, and re-layouts  693 us (36%)
  blocking collectives  290 us (15%)
  matrix products  111 us (6%)
  other arithmetic  65.6 us (3%)
  starting transfers between devices  21.1 us (1%)
    gather x22, local copies, waits for them, and re-layouts, pick_rows(): return jnp.take_along_axis(row_data, row_index[:, :, None], axis=1)  493 us
    unnamed x22, waiting for transfers between devices  247 us
    psum x1, waiting for transfers between devices, on_device(): first_sum, inner_bias_grad = lax.psum((first_part, inner_bias_full), 'mp')  120 us
    psum x1, waiting for transfers between devices, forward(): ffn_out = lax.psum(ffn_terms, 'mp') + bias_float[3]  120 us
    reduce_scatter x1, waiting for transfers between devices, on_device(): lax.psum_scatter(grad_inner_w, 'dp', scatter_dimension=0, tiled=True)  72.4 us
    reduce_scatter x1, waiting for transfers between devices, on_device(): lax.psum_scatter(grad_outer_w, 'dp', scatter_dimension=1, tiled=True)  64.7 us
    psum x1, waiting for transfers between devices, forward(): branch = lax.psum(attn_terms, 'mp') + bias_float[2]  55 us
    gather x3, local copies, waits for them, and re-layouts, on_device(): local_slot = jnp.take_along_axis(cluster_perm % tokens, sorting, axis=1)  52.2 us
  transfers between devices with their start and end apart: 19, of which 10 were waited for; matrix products, arithmetic and copies ran while one was open for 16% of the time, Pallas kernels for 0%

commit v1 on v0

v1 whole, which is shorter than its diff:
```python
from functools import partial
import math

import jax
import jax.numpy as jnp
from jax import lax
from jax.experimental import pallas as pl
from jax.experimental.pallas import tpu as pltpu
from jax.sharding import PartitionSpec as P

D = 768
HEAD_DIM = 64
FF = 3072
CLUSTER = 128
LANES = 128
EPSILON = 1e-05
MASKED = -1e30
SCALE = 1.0 / math.sqrt(HEAD_DIM)

bf16 = jnp.bfloat16
f32 = jnp.float32
i32 = jnp.int32


def nn(a, b):
    return lax.dot_general(a, b, (((1,), (0,)), ((), ())), preferred_element_type=f32)


def nt(a, b):
    return lax.dot_general(a, b, (((1,), (1,)), ((), ())), preferred_element_type=f32)


def tn(a, b):
    return lax.dot_general(a, b, (((0,), (0,)), ((), ())), preferred_element_type=f32)


def lane_iota(rows, lanes=LANES):
    return lax.broadcasted_iota(i32, (rows, lanes), 1)


def sublane_iota(rows, lanes=LANES):
    return lax.broadcasted_iota(i32, (rows, lanes), 0)


def as_column(row):
    parts = [
        jnp.broadcast_to(row[:, i * LANES : (i + 1) * LANES], (LANES, LANES)).T
        for i in range(row.shape[1] // LANES)
    ]
    return parts[0] if len(parts) == 1 else jnp.concatenate(parts, axis=0)


class Layout:
    def __init__(self, peers, tokens, heads):
        self.peers, self.tokens, self.heads = peers, tokens, heads
        self.stripe = min(16, peers)
        self.runs = peers // self.stripe
        self.per_dev = CLUSTER // self.stripe
        self.rows_peer = tokens // peers
        self.half_rows = self.rows_peer // 2
        self.pairs = self.half_rows // self.per_dev
        self.packed = tokens // 2
        self.clusters = peers * tokens // CLUSTER
        self.peers_chunk = 256 // self.half_rows
        self.data_rows = 9 * self.half_rows


def place_kernel(lay, perm_ref, code_ref):
    groups = lay.clusters
    strict = (sublane_iota(LANES) > lane_iota(LANES)).astype(f32).astype(bf16)
    shift = CLUSTER.bit_length() - 1
    blocks = lay.tokens // LANES
    for h in range(lay.heads):

        def members(b):
            row = perm_ref[h : h + 1, pl.ds(pl.multiple_of(b * LANES, LANES), LANES)]
            column = as_column(lax.shift_right_logical(row, shift))
            wide = jnp.concatenate([column] * (groups // LANES), axis=1)
            return (wide == lane_iota(LANES, groups)).astype(f32)

        if lay.runs == 1:
            base = (lane_iota(1, groups) * lay.per_dev).astype(f32)
        else:
            counts = lax.fori_loop(
                0,
                blocks,
                lambda b, c: c + jnp.sum(members(b), axis=0, keepdims=True),
                jnp.zeros((1, groups), f32),
            )
            before = (sublane_iota(groups, groups) < lane_iota(groups, groups)).astype(f32)
            base = nn(jnp.broadcast_to(counts, (16, groups)).astype(bf16), before.astype(bf16))[:1]

        def step(b, carry):
            member = members(b)
            ahead = nn(strict, member.astype(bf16)) + carry
            rank = jnp.sum(member * ahead, axis=1, keepdims=True).astype(i32)
            peer = rank // lay.rows_peer
            rest = rank - peer * lay.rows_peer
            half = (rest >= lay.half_rows).astype(i32)
            packed = peer * lay.half_rows + rest - half * lay.half_rows
            lane = lane_iota(LANES)
            code = jnp.where(lane == 0, packed, jnp.where(lane == 1, half, 0))
            code_ref[h, :, pl.ds(pl.multiple_of(b * LANES, LANES), LANES)] = code.T[:8]
            return carry + jnp.sum(member, axis=0, keepdims=True)

        lax.fori_loop(0, blocks, step, base)


def place_tokens(lay, perm):
    return pl.pallas_call(
        partial(place_kernel, lay),
        out_shape=jax.ShapeDtypeStruct((lay.heads, 8, lay.tokens), i32),
        name="place_tokens",
    )(perm)


def scatter_matrix(code_ref, h, first, rows, tokens):
    packed = code_ref[h, 0:1, :]
    wanted = sublane_iota(rows, tokens) + first
    return jnp.where(jnp.broadcast_to(packed, (rows, tokens)) == wanted, 1.0, 0.0).astype(bf16)


def gather_matrix(column, packed_rows):
    rows = column.shape[0]
    lane = lane_iota(rows)
    parts = [
        jnp.where(column == lane + k * LANES, 1.0, 0.0).astype(bf16)
        for k in range(packed_rows // LANES)
    ]
    return jnp.concatenate(parts, axis=1)


def project_kernel(lay, x_ref, w_ref, bias_ref, code_ref, pad_ref, out_ref, rows_ref, flag_ref):
    h = pl.program_id(0)
    lane_half = (lane_iota(256) >= HEAD_DIM).astype(i32)

    def project(c, _):
        at = pl.ds(pl.multiple_of(c * 256, 256), 256)
        values = nn(x_ref[at, :], w_ref[...]) + bias_ref[0:1, :]
        half = as_column(code_ref[0, 1:2, at])
        keep = half == lane_half
        for x in range(3):
            part = values[:, x * LANES : (x + 1) * LANES]
            rows_ref[at, x * LANES : (x + 1) * LANES] = jnp.where(keep, part, 0.0).astype(bf16)
        live = as_column(pad_ref[0:1, at])
        flags = jnp.where((lane_iota(256) == half) & (live == 1), 1.0, 0.0)
        rows_ref[at, 3 * LANES :] = flags.astype(bf16)
        return 0

    lax.fori_loop(0, lay.tokens // 256, project, 0)

    def sort(j, _):
        chosen = scatter_matrix(code_ref, 0, j * 256, 256, lay.tokens)
        moved = nn(chosen, rows_ref[...])
        peers = pl.ds(j * lay.peers_chunk, lay.peers_chunk)
        for x in range(3):
            part = moved[:, x * LANES : (x + 1) * LANES]
            part = part.reshape(lay.peers_chunk, lay.half_rows, LANES).astype(bf16)
            first = pl.multiple_of((h * 3 + x) * lay.half_rows, 16)
            out_ref[peers, pl.ds(first, lay.half_rows), :] = part
        flags = moved[:, 3 * LANES :]
        for i in range(2):
            at = pl.ds(pl.multiple_of(j * 256 + i * LANES, LANES), LANES)
            flag_ref[h, :, at] = flags[i * LANES : (i + 1) * LANES, :].T[:8]
        return 0

    lax.fori_loop(0, lay.packed // 256, sort, 0)

    @pl.when(h == lay.heads - 1)
    def _():
        for p in range(lay.peers):
            at = slice(p * lay.half_rows, (p + 1) * lay.half_rows)
            rows = [flag_ref[k, 0:2, at] for k in range(lay.heads)]
            block = jnp.concatenate(rows + [jnp.zeros((16 - 2 * lay.heads, lay.half_rows), f32)], axis=0)
            if lay.half_rows < LANES:
                block = jnp.concatenate(
                    [block, jnp.zeros((16, LANES - lay.half_rows), f32)], axis=1
                )
            out_ref[p, lay.data_rows : lay.data_rows + 16, :] = block.astype(bf16)


def project_rows(lay, x, weights, bias, code, pad):
    width = 3 * LANES
    return pl.pallas_call(
        partial(project_kernel, lay),
        grid=(lay.heads,),
        in_specs=[
            pl.BlockSpec((lay.tokens, D), lambda h: (0, 0)),
            pl.BlockSpec((D, width), lambda h: (0, h)),
            pl.BlockSpec((1, width), lambda h: (0, h)),
            pl.BlockSpec((1, 8, lay.tokens), lambda h: (h, 0, 0)),
            pl.BlockSpec((1, lay.tokens), lambda h: (0, 0)),
        ],
        out_specs=pl.BlockSpec((lay.peers, lay.data_rows + 16, LANES), lambda h: (0, 0, 0)),
        out_shape=jax.ShapeDtypeStruct((lay.peers, lay.data_rows + 16, LANES), bf16),
        scratch_shapes=[
            pltpu.VMEM((lay.tokens, 4 * LANES), bf16),
            pltpu.VMEM((lay.heads, 8, lay.packed), f32),
        ],
        name="project_rows",
    )(x, weights, bias, code, pad)


def pair_rows(lay, ref, first, run, p):
    block = ref[run * lay.stripe : (run + 1) * lay.stripe, first : first + lay.half_rows, :]
    if lay.per_dev % 16:
        block = block.astype(f32)
    block = block[:, p * lay.per_dev : (p + 1) * lay.per_dev, :]
    return block.reshape(CLUSTER, LANES).astype(bf16)


def put_pair(lay, ref, first, run, p, rows):
    at = slice(first + p * lay.per_dev, first + (p + 1) * lay.per_dev)
    rows = rows.reshape(lay.stripe, lay.per_dev, LANES).astype(ref.dtype)
    ref[run * lay.stripe : (run + 1) * lay.stripe, at, :] = rows


def live_rows(lay, flag_ref, h):
    flags = flag_ref[...].astype(f32)
    row = lax.broadcasted_iota(i32, flags.shape, 1)
    wide = lay.pairs * LANES
    lane = lane_iota(LANES, wide)
    inner = lane % LANES
    source = (lane // LANES) * lay.per_dev + inner % lay.per_dev
    spread = jnp.where(sublane_iota(LANES, wide) == source, 1.0, 0.0).astype(bf16)
    out = []
    for half in range(2):
        chosen = jnp.sum(jnp.where(row == 2 * h + half, flags, 0.0), axis=1)
        if lay.peers < 16:
            chosen = jnp.concatenate([chosen, jnp.zeros((16 - lay.peers, LANES), f32)], axis=0)
        moved = nn(chosen.astype(bf16), spread)
        rows = []
        for run in range(lay.runs):
            part = moved[run * lay.stripe : (run + 1) * lay.stripe]
            own = (lane_iota(lay.stripe, wide) % LANES) // lay.per_dev == sublane_iota(lay.stripe, wide)
            rows.append(jnp.sum(jnp.where(own, part, 0.0), axis=0, keepdims=True))
        out.append(rows)
    return out


def split_lanes(rows):
    low = lane_iota(rows.shape[0], rows.shape[1]) < HEAD_DIM
    zero = jnp.zeros_like(rows)
    return jnp.where(low, rows, zero), jnp.where(low, zero, rows)


def soft_weights(queries, keys, live):
    scores = nt(queries, keys) * SCALE
    allowed = (live > 0.5) | (lane_iota(CLUSTER) == sublane_iota(CLUSTER))
    scores = jnp.where(allowed, scores, MASKED)
    grown = jnp.exp(scores - jnp.max(scores, axis=1, keepdims=True))
    return grown / jnp.sum(grown, axis=1, keepdims=True)


def attend_kernel(lay, rows_ref, flag_ref, out_ref):
    live = live_rows(lay, flag_ref, pl.program_id(0))
    low = lane_iota(CLUSTER) < HEAD_DIM
    for run in range(lay.runs):
        for p in range(lay.pairs):
            q, k, v = (pair_rows(lay, rows_ref, x * lay.half_rows, run, p) for x in range(3))
            mixed = []
            for half, part in enumerate(split_lanes(q)):
                soft = soft_weights(part, k, live[half][run][:, p * LANES : (p + 1) * LANES])
                mixed.append(nn(soft.astype(bf16), v))
            put_pair(lay, out_ref, 0, run, p, jnp.where(low, mixed[0], mixed[1]))


def exchange_specs(lay):
    return (
        pl.BlockSpec((lay.peers, 3 * lay.half_rows, LANES), lambda h: (0, h, 0)),
        pl.BlockSpec((lay.peers, 16, LANES), lambda h: (0, lay.data_rows // 16, 0)),
        pl.BlockSpec((lay.peers, lay.half_rows, LANES), lambda h: (0, h, 0)),
    )


def attend(lay, arrived):
    rows, flags, single = exchange_specs(lay)
    return pl.pallas_call(
        partial(attend_kernel, lay),
        grid=(lay.heads,),
        in_specs=[rows, flags],
        out_specs=single,
        out_shape=jax.ShapeDtypeStruct((lay.peers, lay.heads * lay.half_rows, LANES), bf16),
        name="attend",
    )(arrived, arrived)


def attend_back_kernel(lay, rows_ref, flag_ref, grad_ref, out_ref, sum_ref):
    live = live_rows(lay, flag_ref, pl.program_id(0))
    low = lane_iota(CLUSTER) < HEAD_DIM
    sums = [jnp.zeros((1, LANES), f32)] * 2
    for run in range(lay.runs):
        for p in range(lay.pairs):
            q, k, v = (pair_rows(lay, rows_ref, x * lay.half_rows, run, p) for x in range(3))
            g = pair_rows(lay, grad_ref, 0, run, p)
            parts = []
            for half, (qh, gh) in enumerate(zip(split_lanes(q), split_lanes(g))):
                soft = soft_weights(qh, k, live[half][run][:, p * LANES : (p + 1) * LANES])
                grad_soft = nt(gh, v)
                delta = jnp.sum(soft * grad_soft, axis=1, keepdims=True)
                grad = (soft * (grad_soft - delta)).astype(bf16)
                parts.append((nn(grad, k), tn(grad, q), tn(soft.astype(bf16), g)))
            one, two = parts
            grad_q = (jnp.where(low, one[0], two[0]) * SCALE).astype(bf16)
            grad_k = (jnp.where(low, one[1], two[1]) * SCALE).astype(bf16)
            grad_v = jnp.where(low, one[2], two[2]).astype(bf16)
            for x, rows in enumerate((grad_q, grad_k, grad_v)):
                put_pair(lay, out_ref, x * lay.half_rows, run, p, rows)
            sums[0] = sums[0] + jnp.sum(grad_q.astype(f32), axis=0, keepdims=True)
            sums[1] = sums[1] + jnp.sum(grad_v.astype(f32), axis=0, keepdims=True)
    sum_ref[0] = jnp.concatenate(sums + [jnp.zeros((6, LANES), f32)], axis=0)


def attend_back(lay, arrived, grads):
    rows, flags, single = exchange_specs(lay)
    return pl.pallas_call(
        partial(attend_back_kernel, lay),
        grid=(lay.heads,),
        in_specs=[rows, flags, single],
        out_specs=[rows, pl.BlockSpec((1, 8, LANES), lambda h: (h, 0, 0))],
        out_shape=[
            jax.ShapeDtypeStruct((lay.peers, lay.data_rows, LANES), bf16),
            jax.ShapeDtypeStruct((lay.heads, 8, LANES), f32),
        ],
        name="attend_back",
    )(arrived, arrived, grads)


def unsort_kernel(lay, rows_ref, code_ref, out_ref):
    rows = rows_ref[...].reshape(lay.packed, LANES)
    low = lane_iota(256) < HEAD_DIM

    def quarter(q, _):
        sides = []
        for side in range(2):
            at = pl.ds(pl.multiple_of(q * 512 + side * 256, 256), 256)
            column = as_column(code_ref[0, 0:1, at])
            half = as_column(code_ref[0, 1:2, at])
            found = nn(gather_matrix(column, lay.packed), rows)
            sides.append(jnp.where(half == side, found, pltpu.roll(found, HEAD_DIM, 1)))
        out_ref[q] = jnp.where(low, sides[0], sides[1]).astype(bf16)
        return 0

    lax.fori_loop(0, lay.tokens // 512, quarter, 0)


def unsort_rows(lay, returned, code):
    quarters = lay.tokens // 512
    return pl.pallas_call(
        partial(unsort_kernel, lay),
        grid=(lay.heads,),
        in_specs=[
            pl.BlockSpec((lay.peers, lay.half_rows, LANES), lambda h: (0, h, 0)),
            pl.BlockSpec((1, 8, lay.tokens), lambda h: (h, 0, 0)),
        ],
        out_specs=pl.BlockSpec((quarters, 256, LANES), lambda h: (0, 0, h)),
        out_shape=jax.ShapeDtypeStruct((quarters, 256, lay.heads * LANES), bf16),
        name="unsort_rows",
    )(returned, code)


def sort_kernel(lay, grad_ref, code_ref, out_ref, rows_ref):
    low = lane_iota(256) < HEAD_DIM
    lane_half = (lane_iota(256) >= HEAD_DIM).astype(i32)

    def quarter(q, _):
        block = grad_ref[q].astype(f32)
        turned = pltpu.roll(block, HEAD_DIM, 1)
        for side in range(2):
            at = pl.ds(pl.multiple_of(q * 512 + side * 256, 256), 256)
            half = as_column(code_ref[0, 1:2, at])
            both = jnp.where(low, block, turned) if side == 0 else jnp.where(low, turned, block)
            rows_ref[at, :] = jnp.where(half == lane_half, both, 0.0).astype(bf16)
        return 0

    lax.fori_loop(0, lay.tokens // 512, quarter, 0)

    def sort(j, _):
        chosen = scatter_matrix(code_ref, 0, j * 256, 256, lay.tokens)
        moved = nn(chosen, rows_ref[...]).astype(bf16)
        peers = pl.ds(j * lay.peers_chunk, lay.peers_chunk)
        out_ref[peers] = moved.astype(f32).reshape(lay.peers_chunk, lay.half_rows, LANES).astype(bf16)
        return 0

    lax.fori_loop(0, lay.packed // 256, sort, 0)


def sort_rows(lay, grads, code):
    quarters = lay.tokens // 512
    return pl.pallas_call(
        partial(sort_kernel, lay),
        grid=(lay.heads,),
        in_specs=[
            pl.BlockSpec((quarters, 256, LANES), lambda h: (0, 0, h)),
            pl.BlockSpec((1, 8, lay.tokens), lambda h: (h, 0, 0)),
        ],
        out_specs=pl.BlockSpec((lay.peers, lay.half_rows, LANES), lambda h: (0, h, 0)),
        out_shape=jax.ShapeDtypeStruct((lay.peers, lay.heads * lay.half_rows, LANES), bf16),
        scratch_shapes=[pltpu.VMEM((lay.tokens, LANES), bf16)],
        name="sort_rows",
    )(grads, code)


def mean_rows(v):
    return jnp.sum(v, axis=1, keepdims=True) * (1.0 / D)


def norm_forward(rows):
    centred = rows - mean_rows(rows)
    inv = lax.rsqrt(mean_rows(centred * centred) + EPSILON)
    return centred * inv, inv


def norm_backward(scaled, normed, inv):
    return inv * (scaled - mean_rows(scaled) - normed * mean_rows(scaled * normed))


def middle_kernel(
    quarter_ref,
    att_ref,
    hidden_ref,
    cot_ref,
    par_ref,
    wo_ref,
    wf_ref,
    out_ref,
    act_ref,
    pre_ref,
    low_ref,
    ffn_grad_ref,
    branch_grad_ref,
    h1_ref,
    att_grad_ref,
    vec_ref,
    first_ref,
    normed_ref,
    inv_ref,
    slope_ref,
    sum_ref,
    h2_ref,
):
    step = pl.program_id(0)
    parts = att_ref.shape[0]

    @pl.when(step == 0)
    def _():
        vec_ref[...] = jnp.zeros_like(vec_ref)
        for side in range(2):
            branch = jnp.zeros((256, D), f32)
            for m in range(parts):
                att = att_ref[m]
                lane = lane_iota(256, att.shape[1]) % LANES
                own = (lane < HEAD_DIM) if side == 0 else (lane >= HEAD_DIM)
                branch = branch + nt(jnp.where(own, att, jnp.zeros_like(att)), wo_ref[m])
            at = slice(side * 256, side * 256 + 256)
            rows = hidden_ref[at, :].astype(f32) + (branch + par_ref[2:3, :])
            normed, inv = norm_forward(rows)
            first = normed * par_ref[4:5, :] + par_ref[6:7, :]
            first_ref[at, :] = first
            normed_ref[at, :] = normed
            inv_ref[at, :] = jnp.broadcast_to(inv, (256, LANES))
            low_ref[at, :] = first.astype(bf16)
        sum_ref[...] = jnp.zeros_like(sum_ref)

    @pl.when((step >= 1) & (step <= 4))
    def _():
        j = step - 1
        for side in range(2):
            at = slice(side * 256, side * 256 + 256)
            pre = nn(low_ref[at, :], wf_ref[0, :, :D]) + par_ref[pl.ds(8 + j, 1), :]
            cdf = 0.5 * (1.0 + lax.erf(pre * (1.0 / math.sqrt(2.0))))
            slope_ref[j, at, :] = cdf + pre * jnp.exp(-0.5 * pre * pre) * (1.0 / math.sqrt(2.0 * math.pi))
            act = (pre * cdf).astype(bf16)
            act_ref[at, :] = act
            sum_ref[at, :] += nt(act, wf_ref[0, :, D:])

    @pl.when(step == 4)
    def _():
        for side in range(4):
            at = slice(side * 128, side * 128 + 128)
            rows = first_ref[at, :] + (sum_ref[at, :] + par_ref[3:4, :])
            normed, inv = norm_forward(rows)
            out_ref[at, :] = (normed * par_ref[5:6, :] + par_ref[7:8, :]).astype(bf16)
            cot = cot_ref[at, :].astype(f32)
            grad = norm_backward(cot * par_ref[5:6, :], normed, inv)
            grad_low = grad.astype(bf16)
            h2_ref[at, :] = grad
            ffn_grad_ref[at, :] = grad_low
            vec_ref[3:4, :] += jnp.sum(grad_low.astype(f32), axis=0, keepdims=True)
            vec_ref[5:6, :] += jnp.sum(cot * normed, axis=0, keepdims=True)
            vec_ref[7:8, :] += jnp.sum(cot, axis=0, keepdims=True)
        sum_ref[...] = jnp.zeros_like(sum_ref)

    @pl.when(step >= 5)
    def _():
        j = 8 - step
        total = jnp.zeros((1, D), f32)
        for side in range(2):
            at = slice(side * 256, side * 256 + 256)
            grad_act = nn(ffn_grad_ref[at, :], wf_ref[0, :, D:])
            grad_pre = (grad_act * slope_ref[j, at, :]).astype(bf16)
            pre_ref[at, :] = grad_pre
            total = total + jnp.sum(grad_pre.astype(f32), axis=0, keepdims=True)
            sum_ref[at, :] += nt(grad_pre, wf_ref[0, :, :D])
        vec_ref[pl.ds(8 + j, 1), :] = total

    @pl.when(step == 8)
    def _():
        for side in range(4):
            at = slice(side * 128, side * 128 + 128)
            grad_first = h2_ref[at, :] + sum_ref[at, :]
            normed = normed_ref[at, :]
            grad = norm_backward(grad_first * par_ref[4:5, :], normed, inv_ref[at, 0:1])
            grad_low = grad.astype(bf16)
            h1_ref[at, :] = grad
            branch_grad_ref[at, :] = grad_low
            vec_ref[2:3, :] += jnp.sum(grad_low.astype(f32), axis=0, keepdims=True)
            vec_ref[4:5, :] += jnp.sum(grad_first * normed, axis=0, keepdims=True)
            vec_ref[6:7, :] += jnp.sum(grad_first, axis=0, keepdims=True)
        for m in range(parts):
            both = [nn(branch_grad_ref[s * 256 : s * 256 + 256, :], wo_ref[m]) for s in range(2)]
            lane = lane_iota(256, both[0].shape[1]) % LANES
            att_grad_ref[m] = jnp.where(lane < HEAD_DIM, both[0], both[1]).astype(bf16)


def middle(lay, quarter, att, hidden, cotangent, params, weights):
    parts, _, width = att.shape
    rows = 512

    def up(s, q):
        return (0, jnp.clip(s - 1, 0, 3))

    def down(s, q):
        return (0, jnp.clip(8 - s, 0, 3))

    def both(s, q):
        return (jnp.where(s <= 4, jnp.clip(s - 1, 0, 3), 8 - s), 0, 0)

    def whole(rank):
        return lambda s, q: (0,) * rank

    spec = pltpu.PrefetchScalarGridSpec(
        num_scalar_prefetch=1,
        grid=(9,),
        in_specs=[
            pl.BlockSpec((parts, 256, width), whole(3)),
            pl.BlockSpec((rows, D), lambda s, q: (q[0], 0)),
            pl.BlockSpec((rows, D), lambda s, q: (q[0], 0)),
            pl.BlockSpec((16, D), whole(2)),
            pl.BlockSpec((parts, D, width), lambda s, q: (0, 0, 4)),
            pl.BlockSpec((1, D, 2 * D), both),
        ],
        out_specs=[
            pl.BlockSpec((rows, D), whole(2)),
            pl.BlockSpec((rows, D), up),
            pl.BlockSpec((rows, D), down),
            pl.BlockSpec((rows, D), whole(2)),
            pl.BlockSpec((rows, D), whole(2)),
            pl.BlockSpec((rows, D), whole(2)),
            pl.BlockSpec((rows, D), whole(2)),
            pl.BlockSpec((parts, 256, width), whole(3)),
            pl.BlockSpec((16, D), whole(2)),
        ],
        scratch_shapes=[
            pltpu.VMEM((rows, D), f32),
            pltpu.VMEM((rows, D), f32),
            pltpu.VMEM((rows, LANES), f32),
            pltpu.VMEM((4, rows, D), f32),
            pltpu.VMEM((rows, D), f32),
            pltpu.VMEM((rows, D), f32),
        ],
    )
    return pl.pallas_call(
        middle_kernel,
        grid_spec=spec,
        out_shape=[
            jax.ShapeDtypeStruct((rows, D), bf16),
            jax.ShapeDtypeStruct((rows, FF), bf16),
            jax.ShapeDtypeStruct((rows, FF), bf16),
            jax.ShapeDtypeStruct((rows, D), bf16),
            jax.ShapeDtypeStruct((rows, D), bf16),
            jax.ShapeDtypeStruct((rows, D), bf16),
            jax.ShapeDtypeStruct((rows, D), f32),
            jax.ShapeDtypeStruct((parts, 256, width), bf16),
            jax.ShapeDtypeStruct((16, D), f32),
        ],
        compiler_params=pltpu.CompilerParams(vmem_limit_bytes=60 * 1024 * 1024),
        name="middle",
    )(quarter, att, hidden, cotangent, params, weights, weights)


def weight_grad_kernel(act_ref, pre_ref, low_ref, ffn_ref, branch_ref, att_ref, out_ref):
    out_ref[:, :D] = tn(low_ref[...], pre_ref[...]).astype(bf16)
    out_ref[:, D : 2 * D] = tn(ffn_ref[...], act_ref[...]).astype(bf16)
    low, high = att_ref[0], att_ref[0]
    lane = lane_iota(256, low.shape[1]) % LANES
    low = jnp.where(lane < HEAD_DIM, low, jnp.zeros_like(low))
    high = jnp.where(lane < HEAD_DIM, jnp.zeros_like(high), high)
    out_ref[:, 2 * D :] = (tn(branch_ref[:256, :], low) + tn(branch_ref[256:, :], high)).astype(bf16)


def weight_grads(act, pre, low, ffn_grad, branch_grad, att):
    parts, _, width = att.shape
    rows = act.shape[0]
    total = 2 * D + width
    whole = pl.BlockSpec((rows, D), lambda j: (0, 0))
    return pl.pallas_call(
        weight_grad_kernel,
        grid=(parts,),
        in_specs=[
            pl.BlockSpec((rows, D), lambda j: (0, j)),
            pl.BlockSpec((rows, D), lambda j: (0, j)),
            whole,
            whole,
            whole,
            pl.BlockSpec((1, 256, width), lambda j: (j, 0, 0)),
        ],
        out_specs=pl.BlockSpec((D, total), lambda j: (j, 0)),
        out_shape=jax.ShapeDtypeStruct((parts * D, total), bf16),
        compiler_params=pltpu.CompilerParams(vmem_limit_bytes=40 * 1024 * 1024),
        name="weight_grads",
    )(act, pre, low, ffn_grad, branch_grad, att)


def collect_kernel(lay, rows_ref, code_ref, x_ref, w_ref, hidden_ref, grad_ref, total_ref):
    chunk = pl.program_id(0)
    low = lane_iota(256) < HEAD_DIM
    firsts, seconds = [], []
    for h in range(lay.heads):
        column = as_column(code_ref[h, 0:1, :])
        half = as_column(code_ref[h, 1:2, :])
        planes = [
            rows_ref[:, (h * 3 + x) * lay.half_rows : (h * 3 + x + 1) * lay.half_rows, :].reshape(
                lay.packed, LANES
            )
            for x in range(3)
        ]
        found = nn(gather_matrix(column, lay.packed), jnp.concatenate(planes, axis=1))
        one, two = [], []
        for x in range(3):
            part = found[:, x * LANES : (x + 1) * LANES]
            turned = pltpu.roll(part, HEAD_DIM, 1)
            one.append(jnp.where(half == 0, part, turned))
            two.append(jnp.where(half == 1, part, turned))
        firsts.append(one)
        seconds.append(two)
    tiles = [jnp.where(low, firsts[h][0], seconds[h][1]) for h in range(lay.heads)]
    for h in range(0, lay.heads, 2):
        right = seconds[h + 1][2] if h + 1 < lay.heads else jnp.zeros((256, LANES), f32)
        tiles.append(jnp.where(low, firsts[h][2], right))
    dense = jnp.concatenate(tiles, axis=1).astype(bf16)
    hidden_ref[...] = nt(dense, w_ref[...]).astype(bf16)
    part = tn(x_ref[...], dense)

    @pl.when(chunk == 0)
    def _():
        total_ref[...] = part

    @pl.when(chunk > 0)
    def _():
        total_ref[...] += part

    @pl.when(chunk == pl.num_programs(0) - 1)
    def _():
        grad_ref[...] = total_ref[...].astype(bf16)


def collect(lay, returned, code, x, weights):
    width = weights.shape[1]
    return pl.pallas_call(
        partial(collect_kernel, lay),
        grid=(lay.tokens // 256,),
        in_specs=[
            pl.BlockSpec((lay.peers, lay.data_rows, LANES), lambda c: (0, 0, 0)),
            pl.BlockSpec((lay.heads, 8, 256), lambda c: (0, 0, c)),
            pl.BlockSpec((256, D), lambda c: (c, 0)),
            pl.BlockSpec((D, width), lambda c: (0, 0)),
        ],
        out_specs=[
            pl.BlockSpec((256, D), lambda c: (c, 0)),
            pl.BlockSpec((D, width), lambda c: (0, 0)),
        ],
        out_shape=[
            jax.ShapeDtypeStruct((lay.tokens, D), bf16),
            jax.ShapeDtypeStruct((D, width), bf16),
        ],
        scratch_shapes=[pltpu.VMEM((D, width), f32)],
        compiler_params=pltpu.CompilerParams(vmem_limit_bytes=40 * 1024 * 1024),
        name="collect",
    )(returned, code, x, weights)


def over_rows(rows):
    return lax.all_to_all(rows, "dp", split_axis=0, concat_axis=0, tiled=True)


def over_heads(rows):
    return lax.all_to_all(rows, "mp", split_axis=0, concat_axis=0, tiled=True)


def swap(rows, flip):
    return lax.ppermute(rows, "mp", [(i, i ^ flip) for i in range(lax.axis_size("mp"))])


def share_quarters(rows, place):
    whole = jnp.zeros((4,) + rows.shape, rows.dtype)
    other = swap(rows, 2)
    two = jnp.stack([rows, other])
    four = swap(two, 1)
    whole = lax.dynamic_update_index_in_dim(whole, rows, place, 0)
    whole = lax.dynamic_update_index_in_dim(whole, other, place ^ 2, 0)
    whole = lax.dynamic_update_index_in_dim(whole, four[0], place ^ 1, 0)
    whole = lax.dynamic_update_index_in_dim(whole, four[1], place ^ 3, 0)
    return whole.reshape((4 * rows.shape[0],) + rows.shape[1:])


def add_quarters(rows, place):
    size = rows.shape[0] // 4
    grid = rows.reshape(2, 2, size, rows.shape[1])
    core, far = place % 2, place // 2
    mine = lax.dynamic_index_in_dim(grid, core, 1, keepdims=False)
    theirs = lax.dynamic_index_in_dim(grid, 1 - core, 1, keepdims=False)
    chip = mine.astype(f32) + swap(theirs, 1).astype(f32)
    send = lax.dynamic_index_in_dim(chip, 1 - far, 0, keepdims=False).astype(bf16)
    keep = lax.dynamic_index_in_dim(chip, far, 0, keepdims=False)
    return keep + swap(send, 2).astype(f32)


def on_device(
    hidden_in,
    cotangent,
    w_query,
    w_key,
    w_value,
    w_output,
    w_inner,
    w_outer,
    biases,
    gains,
    shifts,
    inner_bias,
    lengths,
    padding,
    cluster_perm,
):
    peers = lax.axis_size("dp")
    tokens = hidden_in.shape[0]
    heads = cluster_perm.shape[0]
    lay = Layout(peers, tokens, heads)
    place = lax.axis_index("mp")
    row_block = lax.axis_index("dp")
    depth = w_query.shape[0]
    head_width = heads * HEAD_DIM

    out_t = jnp.broadcast_to(
        w_output.T.reshape(depth, heads, 1, HEAD_DIM), (depth, heads, 2, HEAD_DIM)
    ).reshape(depth, heads * LANES)
    shard = jnp.concatenate([w_inner, w_outer.T, out_t], axis=1)
    middle_w = lax.all_gather(shard, ("mp", "dp"), axis=0, tiled=True).reshape(4, D, -1)

    small = jnp.concatenate(
        [biases, gains, shifts, inner_bias.reshape(4, depth)], axis=0
    )
    width = 3 * head_width
    per_head = jnp.concatenate(
        [w.reshape(depth, heads, 1, HEAD_DIM) for w in (w_query, w_key, w_value)], axis=2
    ).reshape(depth, width)
    tail = small.reshape(-1)
    tail_rows = -(-tail.shape[0] // width)
    tail = jnp.pad(tail, (0, tail_rows * width - tail.shape[0])).reshape(tail_rows, width)
    got = lax.all_gather(jnp.concatenate([per_head, tail], axis=0), "dp", axis=0, tiled=False)
    weights = got[:, :depth].reshape(D, heads, 3, HEAD_DIM)
    vectors = got[:, depth:].reshape(peers, -1)[:, : 12 * depth].astype(f32)
    params = vectors.reshape(peers, 12, depth)[:, :8].transpose(1, 0, 2).reshape(8, D)
    inner = vectors.reshape(peers, 12, depth)[:, 8:].reshape(4, D)
    params = jnp.concatenate([params, inner, jnp.zeros((4, D), f32)], axis=0)
    doubled = jnp.broadcast_to(
        weights[:, :, :, None, :], (D, heads, 3, 2, HEAD_DIM)
    ).reshape(D, heads * 3 * LANES)
    own = lax.dynamic_slice_in_dim(params[:2], place * head_width, head_width, 1)
    own = own.reshape(2, heads, HEAD_DIM)
    own = jnp.stack([own[0], jnp.zeros_like(own[0]), own[1]], axis=1)
    own = jnp.broadcast_to(own[:, :, None, :], (heads, 3, 2, HEAD_DIM)).reshape(1, -1)

    code = place_tokens(lay, cluster_perm)
    sent = project_rows(lay, hidden_in, doubled, own, code, padding.reshape(1, tokens))
    arrived = over_rows(sent)
    mixed = attend(lay, arrived)
    att = over_heads(unsort_rows(lay, over_rows(mixed), code))
    (
        out_quarter,
        act,
        pre_grad,
        first_low,
        ffn_grad,
        branch_grad,
        grad_h1,
        att_grad,
        vec,
    ) = middle(lay, place.reshape(1), att, hidden_in, cotangent, params, middle_w)

    packed = weight_grads(act, pre_grad, first_low, ffn_grad, branch_grad, att)
    reduced = lax.psum_scatter(packed, ("mp", "dp"), scatter_dimension=0, tiled=True).astype(f32)
    hidden_out = share_quarters(out_quarter, place)

    grads = over_rows(sort_rows(lay, over_heads(att_grad), code))
    slot_grads, bias_sums = attend_back(lay, arrived, grads)

    head_sums = bias_sums[:, :2].reshape(heads, 2, 2, HEAD_DIM).sum(axis=2)
    head_sums = head_sums.transpose(1, 0, 2).reshape(2, head_width)
    vec = lax.dynamic_update_slice(vec[:12], head_sums, (0, place * head_width))
    vec = lax.psum(vec, ("dp", "mp"))

    ordered = jnp.concatenate(
        [
            weights[:, :, :2].reshape(D, 2 * head_width),
            weights[:, :, 2].reshape(D, head_width),
            jnp.zeros((D, (-width) % LANES), bf16),
        ],
        axis=1,
    )
    hidden_part, head_grad = collect(lay, over_rows(slot_grads), code, hidden_in, ordered)
    grad_hidden = share_quarters((add_quarters(hidden_part, place) + grad_h1).astype(bf16), place)

    terms = over_rows(head_grad.reshape(peers, depth, -1))
    total = jnp.sum(terms.astype(f32), axis=0)
    query_key = total[:, : 2 * head_width].reshape(depth, heads, 2, HEAD_DIM)
    grad_query = query_key[:, :, 0].reshape(depth, head_width)
    grad_key = query_key[:, :, 1].reshape(depth, head_width)
    grad_value = total[:, 2 * head_width : width]

    grad_out = reduced[:, 2 * D :].reshape(depth, heads, 2, HEAD_DIM).sum(axis=2)
    small = lax.dynamic_slice_in_dim(vec[:8], row_block * depth, depth, 1)
    grad_inner_bias = lax.dynamic_slice_in_dim(
        vec[8:].reshape(FF), row_block * (FF // peers), FF // peers, 0
    )
    return (
        hidden_out,
        grad_hidden,
        grad_query,
        grad_key,
        grad_value,
        grad_out.reshape(depth, head_width).T,
        reduced[:, :D],
        reduced[:, D : 2 * D].T,
        small[:4],
        small[4:6],
        small[6:8],
        grad_inner_bias,
    )


def solution(mesh):
    placed = (
        P("dp", None),
        P("dp", None),
        P("dp", "mp"),
        P("dp", "mp"),
        P("dp", "mp"),
        P("mp", "dp"),
        P("dp", "mp"),
        P("mp", "dp"),
        P(None, "dp"),
        P(None, "dp"),
        P(None, "dp"),
        P("dp"),
        P(),
        P("dp"),
        P("mp", "dp"),
    )
    return jax.shard_map(
        on_device,
        mesh=mesh,
        in_specs=placed,
        out_specs=(
            P("dp", None),
            P("dp", None),
            P("dp", "mp"),
            P("dp", "mp"),
            P("dp", "mp"),
            P("mp", "dp"),
            P("dp", "mp"),
            P("mp", "dp"),
            P(None, "dp"),
            P(None, "dp"),
            P(None, "dp"),
            P("dp"),
        ),
        check_vma=False,
    )
```

time: 1940 us -> 566 us (0.29)
  local copies, waits for them, and re-layouts: 693 us -> 56.6 us
  waiting for transfers between devices: 727 us -> 102 us
  Pallas kernels: 0 us -> 159 us
  matrix products: 111 us -> 0 us
  blocking collectives: 290 us -> 200 us
  other arithmetic: 65.6 us -> 17.5 us
    gather x29 -> x0, local copies, waits for them, and re-layouts: 614 us -> none  [the longest x22 493 us: pick_rows(): return jnp.take_along_axis(row_data, row_index[:, :, None], axis=1)]
    psum x4 -> x0, waiting for transfers between devices: 295 us -> none  [the longest x1 120 us: on_device(): first_sum, inner_bias_grad = lax.psum((first_part, inner_bias_full), 'mp')]
    unnamed x22 -> x2, waiting for transfers between devices: 247 us -> 0.03 us
    all_gather x8 -> x1, blocking collectives: 217 us -> 36.3 us  [on_device(): lax.all_gather(jnp.concatenate([per_head, tail], axis=0), 'dp', axis=0, t...]
    pallas_call x0 -> x9, Pallas kernels: none -> 159 us  [the longest x1 27 us: middle(): pl.pallas_call(middle_kernel, grid_spec=spec, out_shape=[jax.ShapeDtypeSt...]
    reduce_scatter x2 -> x1, waiting for transfers between devices: 137 us -> 0.01 us  [on_device(): lax.psum_scatter(packed, ('mp', 'dp'), scatter_dimension=0, tiled=True)]
    dot_general x23 -> x0, matrix products: 106 us -> none  [the longest x1 19.8 us: forward(): jnp.dot(first_low, inner_w, preferred_element_type=jnp.float32)]
    all_to_all x1 -> x4, blocking collectives: 25.4 us -> 125 us  [the longest x3 110 us: over_rows(): return lax.all_to_all(rows, 'dp', split_axis=0, concat_axis=0, tiled=True)]
  transfers between devices with their start and end apart: 19 -> 11, of which waited for: 10 -> 6; matrix products, arithmetic and copies ran while one was open for 16% -> 9% of each run, Pallas kernels for 0% -> 22%
where the time goes in v1:
time: 566 us; the launch traced here: 564 us
  blocking collectives  200 us (35%)
  Pallas kernels  159 us (28%)
  waiting for transfers between devices  102 us (18%)
  local copies, waits for them, and re-layouts  56.6 us (10%)
  other arithmetic  17.5 us (3%)
  starting transfers between devices  15.3 us (3%)
  between operations  14.4 us (3%)
    all_to_all x3, blocking collectives, over_rows(): return lax.all_to_all(rows, 'dp', split_axis=0, concat_axis=0, tiled=True)  110 us
    all_to_all x2, waiting for transfers between devices, over_rows(): return lax.all_to_all(rows, 'dp', split_axis=0, concat_axis=0, tiled=True)  48.4 us
    ppermute x6, waiting for transfers between devices, swap(): lax.ppermute(rows, 'mp', [(i, i ^ flip) for i in range(lax.axis_size('mp'...  42.9 us
    psum x1, blocking collectives, on_device(): vec = lax.psum(vec, ('dp', 'mp'))  38.5 us
    all_gather x1, blocking collectives, on_device(): lax.all_gather(jnp.concatenate([per_head, tail], axis=0), 'dp', axis=0, t...  36.3 us
    pallas_call x1, Pallas kernels, middle(): pl.pallas_call(middle_kernel, grid_spec=spec, out_shape=[jax.ShapeDtypeSt...  27 us
    pallas_call x1, Pallas kernels, attend_back(): pl.pallas_call(partial(attend_back_kernel, lay), grid=(lay.heads,), in_sp...  24.6 us
    pallas_call x1, Pallas kernels, project_rows(): pl.pallas_call(partial(project_kernel, lay), grid=(lay.heads,), in_specs=...  21.6 us
  transfers between devices with their start and end apart: 11, of which 6 were waited for; matrix products, arithmetic and copies ran while one was open for 9% of the time, Pallas kernels for 22%

profile of v1, /device:TPU:0, one launch (start us, length us, event | category | flops | bytes accessed | tf_op | source)
XLA Modules:
  0.0 563.8 jit_solution(13538347594495283912)
XLA Ops:
  14.8 36.3 %all-gather.1 = bf16[8,98,576]{2,1,0:T(8,128)(2,1)S(1)} all-gather(bf16[1,98,576]{2,1,0:T(8,128)(2,1)S(1)} %copy.73), channel_id=2, replica_groups=mesh['dp'=8,'mp'=4] {'dp'}, dimensions={0}, use_global_device_ids=true | all-gather | bytes 1016064 | tf_op jit(solution)/shard_map/all_gather | solution.py:771
  55.1 2.2 copy.77.w_ref
  57.3 20.9 %place_tokens.1.code_ref = s32[3,8,2048]{2,1,0:T(8,128)} custom-call(s32[3,2048]{1,0:T(4,128)} %perm_ref.1), custom_call_target="tpu_custom_call" | custom-call | tf_op jit(solution)/shard_map/place_tokens/pallas_call | solution.py:110
  78.3 21.6 %project_rows.1 = bf16[8,1168,128]{2,1,0:T(8,128)(2,1)} custom-call(bf16[2048,768]{1,0:T(8,128)(2,1)} %x_ref.3, bf16[768,1152]{1,0:T(8,128)(2,1)} %copy.77.w_ref, f32[1,1152]{1,0:T(1,128)} %reshape.129.bias_ref, s32[3,8,2048]{2,1,0:T(8,128)} %place_tokens.1.code_ref, s32[1,2048]{1,0:T(1,128)} %bitcast.85), custom_call_target="tpu_custom_call" | custom-call | tf_op jit(solution)/shard_map/project_rows/pallas_call | solution.py:184
  99.8 62.2 %all_to_all.35.rows_ref.flag_ref = bf16[8,1168,128]{2,1,0:T(8,128)(2,1)} all-to-all(bf16[8,1168,128]{2,1,0:T(8,128)(2,1)} %project_rows.1), channel_id=1, replica_groups=mesh['dp'=8,'mp'=4] {'dp'}, dimensions={0} | all-to-all | bytes 4784128 | tf_op jit(solution)/shard_map/all_to_all | solution.py:694
  162.0 17.9 %attend.1 = bf16[8,384,128]{2,1,0:T(8,128)(2,1)} custom-call(bf16[8,1168,128]{2,1,0:T(8,128)(2,1)} %all_to_all.35.rows_ref.flag_ref, bf16[8,1168,128]{2,1,0:T(8,128)(2,1)} %all_to_all.35.rows_ref.flag_ref), custom_call_target="tpu_custom_call" | custom-call | tf_op jit(solution)/shard_map/attend/pallas_call | solution.py:278
  179.9 23.6 %all_to_all.36.rows_ref = bf16[8,384,128]{2,1,0:T(8,128)(2,1)} all-to-all(bf16[8,384,128]{2,1,0:T(8,128)(2,1)} %attend.1), channel_id=1, replica_groups=mesh['dp'=8,'mp'=4] {'dp'}, dimensions={0} | all-to-all | bytes 1572864 | tf_op jit(solution)/shard_map/all_to_all | solution.py:694
  203.5 9.1 %unsort_rows.1 = bf16[4,256,384]{2,1,0:T(8,128)(2,1)} custom-call(bf16[8,384,128]{2,1,0:T(8,128)(2,1)} %all_to_all.36.rows_ref, s32[3,8,2048]{2,1,0:T(8,128)} %place_tokens.1.code_ref), custom_call_target="tpu_custom_call" | custom-call | tf_op jit(solution)/shard_map/unsort_rows/pallas_call | solution.py:349
  212.6 3.5 all-to-all-start.2
  217.3 10.4 %all-to-all-done.2.att_ref = bf16[4,256,384]{2,1,0:T(8,128)(2,1)S(1)} async-done(((bf16[4,256,384]{2,1,0:T(8,128)(2,1)}), bf16[4,256,384]{2,1,0:T(8,128)(2,1)S(1)}, u32[]{:S(2)}, u32[]{:S(2)}) %all-to-all-start.2) | async-done | bytes 786464 | tf_op jit(solution)/shard_map/all_to_all | solution.py:698
  228.7 27.0 %middle.1 = (bf16[512,768]{1,0:T(8,128)(2,1)}, bf16[512,3072]{1,0:T(8,128)(2,1)}, bf16[512,3072]{1,0:T(8,128)(2,1)}, bf16[512,768]{1,0:T(8,128)(2,1)}, bf16[512,...) custom-call(s32[1]{0:T(128)} %bitcast.quarter_ref, ...), custom_call_target="tpu_custom_call" | custom-call | tf_op jit(solution)/shard_map/middle/pallas_call | solution.py:573
  264.0 9.3 %weight_grads.1 = bf16[3072,1920]{1,0:T(8,128)(2,1)} custom-call(bf16[512,3072]{1,0:T(8,128)(2,1)S(1)} %copy-done.6, bf16[512,3072]{1,0:T(8,128)(2,1)S(1)} %copy-done.7, bf16[512,768]{1,0:T(8,128)(2,1)S(1)} %copy-done.8, bf16[512,768]{1,0:T(8,128)(2,1)S(1)} %copy-done.9, bf16[512,768]{1,0:T(8,128)(2,1)S(1)} %copy-done.10, bf16[4,256,384]{2,1,0:T(8,128)(2,1)S(1)} %copy-done.2), custom_call_target="tpu_custom_call" | custom-call | tf_op jit(solution)/shard_map/weight_grads/pallas_call | solution.py:607
  274.5 14.8 %all_to_all.37.grad_ref = bf16[4,256,384]{2,1,0:T(8,128)(2,1)} all-to-all(bf16[4,256,384]{2,1,0:T(8,128)(2,1)S(1)} %copy-done.15), channel_id=1, replica_groups=mesh['dp'=8,'mp'=4] {'mp'}, dimensions={0} | all-to-all | bytes 1572864 | tf_op jit(solution)/shard_map/all_to_all | solution.py:698
  289.3 8.9 %sort_rows.1 = bf16[8,384,128]{2,1,0:T(8,128)(2,1)} custom-call(bf16[4,256,384]{2,1,0:T(8,128)(2,1)} %all_to_all.37.grad_ref, s32[3,8,2048]{2,1,0:T(8,128)} %place_tokens.1.code_ref), custom_call_target="tpu_custom_call" | custom-call | tf_op jit(solution)/shard_map/sort_rows/pallas_call | solution.py:390
  298.2 24.3 %all_to_all.38.grad_ref = bf16[8,384,128]{2,1,0:T(8,128)(2,1)} all-to-all(bf16[8,384,128]{2,1,0:T(8,128)(2,1)} %sort_rows.1), channel_id=1, replica_groups=mesh['dp'=8,'mp'=4] {'dp'}, dimensions={0} | all-to-all | bytes 1572864 | tf_op jit(solution)/shard_map/all_to_all | solution.py:694
  322.5 24.6 %attend_back.1 = (bf16[8,1152,128]{2,1,0:T(8,128)(2,1)}, f32[3,8,128]{2,1,0:T(8,128)}) custom-call(bf16[8,1168,128]{2,1,0:T(8,128)(2,1)} %all_to_all.35.rows_ref.flag_ref, bf16[8,1168,128]{2,1,0:T(8,128)(2,1)} %all_to_all.35.rows_ref.flag_ref, bf16[8,384,128]{2,1,0:T(8,128)(2,1)} %all_to_all.38.grad_ref), custom_call_target="tpu_custom_call" | custom-call | tf_op jit(solution)/shard_map/attend_back/pallas_call | solution.py:316
  347.1 4.4 all-to-all-start.5
  355.3 2.2 copy.80
  359.4 2.4 maximum_maximum_fusion.w_ref
  361.8 48.4 %all-to-all-done.5.rows_ref = bf16[8,1152,128]{2,1,0:T(8,128)(2,1)} async-done(((bf16[8,1152,128]{2,1,0:T(8,128)(2,1)}), bf16[8,1152,128]{2,1,0:T(8,128)(2,1)}, u32[]{:S(2)}, u32[]{:S(2)}) %all-to-all-start.5) | async-done | bytes 2359328 | tf_op jit(solution)/shard_map/all_to_all | solution.py:694
  411.4 19.1 %collect.1 = (bf16[2048,768]{1,0:T(8,128)(2,1)S(1)}, bf16[768,640]{1,0:T(8,128)(2,1)}) custom-call(bf16[8,1152,128]{2,1,0:T(8,128)(2,1)} %all-to-all-done.5.rows_ref, s32[3,8,2048]{2,1,0:T(8,128)S(1)} %copy-done.3, bf16[2048,768]{1,0:T(8,128)(2,1)S(1)} %copy-done, bf16[768,640]{1,0:T(8,128)(2,1)S(1)} %copy-done.4), custom_call_target="tpu_custom_call" | custom-call | tf_op jit(solution)/shard_map/collect/pallas_call | solution.py:670
  432.4 3.5 collective-permute-done.2
  435.9 2.2 convert_add_fusion
  441.1 18.7 %collective-permute-done.3 = bf16[512,768]{1,0:T(8,128)(2,1)} collective-permute-done((bf16[512,768]{1,0:T(8,128)(2,1)}, bf16[512,768]{1,0:T(8,128)(2,1)}, u32[]{:S(2)}, u32[]{:S(2)}) %collective-permute-start.3) | collective-permute-done | bytes 786464 | tf_op jit(solution)/shard_map/ppermute | solution.py:702
  460.0 2.4 constant_dynamic-update-slice_fusion.1
  465.6 3.6 all-to-all-start.6
  469.2 7.5 %collective-permute-done = bf16[512,768]{1,0:T(8,128)(2,1)} collective-permute-done((bf16[512,768]{1,0:T(8,128)(2,1)}, bf16[512,768]{1,0:T(8,128)(2,1)}, u32[]{:S(2)}, u32[]{:S(2)}) %collective-permute-start) | collective-permute-done | bytes 786464 | tf_op jit(solution)/shard_map/ppermute | solution.py:702
  476.6 2.7 pad_maximum_fusion
  479.3 13.3 %collective-permute-done.4 = bf16[512,768]{1,0:T(8,128)(2,1)S(1)} collective-permute-done((bf16[512,768]{1,0:T(8,128)(2,1)}, bf16[512,768]{1,0:T(8,128)(2,1)S(1)}, u32[]{:S(2)}, u32[]{:S(2)}) %collective-permute-start.4) | collective-permute-done | bytes 786464 | tf_op jit(solution)/shard_map/ppermute | solution.py:702
  492.6 2.5 pad_maximum_fusion.1
  501.4 38.5 %psum.7 = f32[12,768]{1,0:T(8,128)S(1)} all-reduce(f32[12,768]{1,0:T(8,128)S(1)} %dynamic_update_slice.36), channel_id=1, replica_groups=mesh['dp'=8,'mp'=4] {'dp','mp'}, use_global_device_ids=true, to_apply=%region_4.5 | all-reduce | flops 9216 | bytes 73728 | tf_op jit(solution)/shard_map/psum | solution.py:812
  545.1 2.6 slice_dynamic-update-slice_fusion.1
  (128 shorter events, 58.9 us)
Async XLA Ops:
  7.2 220.6 %all-gather.4.cloned.1.call-start = ((), (), s32[]{:S(2)}) async-start(), calls=%async_computation.8 | async-start | bytes 12165120 | tf_op jit(solution)/shard_map/all_gather | solution.py:759
  54.9 23.3 %copy-start.11 = (bf16[768,3,3,64]{0,3,2,1:T(8,128)(2,1)}, bf16[768,3,3,64]{0,3,2,1:T(8,128)(2,1)S(1)}, u32[]{:S(2)}) copy-start(bf16[768,3,3,64]{0,3,2,1:T(8,128)(2,1)S(1)} %broadcast_in_dim.43) | copy-start | bytes 2654212
  212.6 15.1 %all-to-all-start.2 = ((bf16[4,256,384]{2,1,0:T(8,128)(2,1)}), bf16[4,256,384]{2,1,0:T(8,128)(2,1)S(1)}, u32[]{:S(2)}, u32[]{:S(2)}) async-start(bf16[4,256,384]{2,1,0:T(8,128)(2,1)} %unsort_rows.1), calls=%async_computation.2 | async-start | bytes 1572864 | tf_op jit(solution)/shard_map/all_to_all | solution.py:698
  216.1 335.7 %reduce-scatter.2.cloned.1.call-start = ((), (), s32[]{:S(2)}) async-start(), calls=%async_computation.9 | async-start | bytes 12165120 | tf_op jit(solution)/shard_map/reduce_scatter | solution.py:803
  227.7 0.9 copy-start.1
  255.7 1.1 copy-start.2
  256.8 1.9 copy-start.6
  258.7 1.9 copy-start.7
  260.6 1.1 copy-start.8
  261.8 1.1 copy-start.9
  262.9 1.1 copy-start.10
  273.4 1.1 copy-start.15
  347.1 63.1 %all-to-all-start.5 = ((bf16[8,1152,128]{2,1,0:T(8,128)(2,1)}), bf16[8,1152,128]{2,1,0:T(8,128)(2,1)}, u32[]{:S(2)}, u32[]{:S(2)}) async-start(bf16[8,1152,128]{2,1,0:T(8,128)(2,1)} %get-tuple-element.27), calls=%async_computation.5 | async-start | bytes 4718592 | tf_op jit(solution)/shard_map/all_to_all | solution.py:694
  351.5 58.7 %copy-start = (bf16[2048,768]{1,0:T(8,128)(2,1)S(1)}, bf16[2048,768]{1,0:T(8,128)(2,1)}, u32[]{:S(2)}) copy-start(bf16[2048,768]{1,0:T(8,128)(2,1)} %x_ref.3) | copy-start | bytes 9437188
  351.5 58.7 %copy-start.3 = (s32[3,8,2048]{2,1,0:T(8,128)S(1)}, s32[3,8,2048]{2,1,0:T(8,128)}, u32[]{:S(2)}) copy-start(s32[3,8,2048]{2,1,0:T(8,128)} %place_tokens.1.code_ref) | copy-start | bytes 589828
  410.2 1.2 copy-start.4
  430.5 1.7 copy-start.5
  432.3 3.6 collective-permute-start.2
  439.1 20.7 %collective-permute-start.3 = (bf16[512,768]{1,0:T(8,128)(2,1)}, bf16[512,768]{1,0:T(8,128)(2,1)}, u32[]{:S(2)}, u32[]{:S(2)}) collective-permute-start(bf16[512,768]{1,0:T(8,128)(2,1)} %fusion.2), channel_id=1, source_target_pairs={{0,2},{1,3},{2,0},{3,1},{4,6},{5,7},{6,4},{7,5},{8,10},{9,11},{10,... | collective-permute-start | bytes 2359304 | tf_op jit(solution)/shard_map/ppermute | solution.py:702
  440.6 19.4 %copy-start.14 = (f32[512,768]{1,0:T(8,128)S(1)}, f32[512,768]{1,0:T(8,128)}, u32[]{:S(2)}) copy-start(f32[512,768]{1,0:T(8,128)} %get-tuple-element.29) | copy-start | bytes 4718596
  440.6 36.0 %collective-permute-start = (bf16[512,768]{1,0:T(8,128)(2,1)}, bf16[512,768]{1,0:T(8,128)(2,1)}, u32[]{:S(2)}, u32[]{:S(2)}) collective-permute-start(bf16[512,768]{1,0:T(8,128)(2,1)} %get-tuple-element.25), channel_id=1, source_target_pairs={{0,2},{1,3},{2,0},{3,1},{4,6},{5,7},{6,4},{7,5},{8,10},{9,11},{10,... | collective-permute-start | bytes 2359304 | tf_op jit(solution)/shard_map/ppermute | solution.py:702
  462.4 1.7 copy-start.12
  464.0 28.6 %collective-permute-start.4 = (bf16[512,768]{1,0:T(8,128)(2,1)}, bf16[512,768]{1,0:T(8,128)(2,1)S(1)}, u32[]{:S(2)}, u32[]{:S(2)}) collective-permute-start(bf16[512,768]{1,0:T(8,128)(2,1)} %get-tuple-element.77), channel_id=1, source_target_pairs={{0,2},{1,3},{2,0},{3,1},{4,6},{5,7},{6,4},{7,5},{8,10},{9,11},{10,... | collective-permute-start | bytes 2359304 | tf_op jit(solution)/shard_map/ppermute | solution.py:702
  465.6 76.2 %all-to-all-start.6 = ((bf16[8,96,640]{2,1,0:T(8,128)(2,1)}), bf16[8,96,640]{2,1,0:T(8,128)(2,1)S(1)}, u32[]{:S(2)}, u32[]{:S(2)}) async-start(bf16[8,96,640]{2,1,0:T(8,128)(2,1)} %bitcast.27), calls=%async_computation.6 | async-start | bytes 1966080 | tf_op jit(solution)/shard_map/all_to_all | solution.py:694
  479.3 65.8 %collective-permute-start.1 = (bf16[2,512,768]{2,1,0:T(8,128)(2,1)}, bf16[2,512,768]{2,1,0:T(8,128)(2,1)}, u32[]{:S(2)}, u32[]{:S(2)}) collective-permute-start(bf16[2,512,768]{2,1,0:T(8,128)(2,1)} %pad_maximum_fusion), channel_id=1, source_target_pairs={{0,1},{1,0},{2,3},{3,2},{4,5},{5,4},{6,7},{7,6},{8,9},{9,8},{10,11... | collective-permute-start | bytes 4718600 | tf_op jit(solution)/shard_map/ppermute | solution.py:702
  492.6 4.4 copy-start.13
  495.1 50.0 %collective-permute-start.5 = (bf16[2,512,768]{2,1,0:T(8,128)(2,1)}, bf16[2,512,768]{2,1,0:T(8,128)(2,1)}, u32[]{:S(2)}, u32[]{:S(2)}) collective-permute-start(bf16[2,512,768]{2,1,0:T(8,128)(2,1)} %pad_maximum_fusion.1), channel_id=1, source_target_pairs={{0,1},{1,0},{2,3},{3,2},{4,5},{5,4},{6,7},{7,6},{8,9},{9,8},{10,11... | collective-permute-start | bytes 4718600 | tf_op jit(solution)/shard_map/ppermute | solution.py:702
  495.1 5.8 %copy-start.16 = (f32[16,768]{1,0:T(8,128)S(1)}, f32[16,768]{1,0:T(8,128)}, u32[]{:S(2)}) copy-start(f32[16,768]{1,0:T(8,128)} %get-tuple-element.36) | copy-start | bytes 147460
Sparse Core Ops, SparseCore 0:
  10.9 108.5 all-gather.3
  273.5 177.0 reduce-scatter.1

commit v2 on v1

v2 whole, which is shorter than its diff:
```python
from functools import partial
import math

import jax
import jax.numpy as jnp
from jax import lax
from jax.experimental import pallas as pl
from jax.experimental.pallas import tpu as pltpu
from jax.sharding import PartitionSpec as P

D = 768
HEAD_DIM = 64
FF = 3072
CLUSTER = 128
LANES = 128
EPSILON = 1e-05
MASKED = -1e30
SCALE = 1.0 / math.sqrt(HEAD_DIM)

bf16 = jnp.bfloat16
f32 = jnp.float32
i32 = jnp.int32

VMEM = 60 * 1024 * 1024
QUICK = pl.CostEstimate(flops=1000, bytes_accessed=1000, transcendentals=0)


def nn(a, b):
    return lax.dot_general(a, b, (((1,), (0,)), ((), ())), preferred_element_type=f32)


def nt(a, b):
    return lax.dot_general(a, b, (((1,), (1,)), ((), ())), preferred_element_type=f32)


def tn(a, b):
    return lax.dot_general(a, b, (((0,), (0,)), ((), ())), preferred_element_type=f32)


def lane_iota(rows, lanes=LANES):
    return lax.broadcasted_iota(i32, (rows, lanes), 1)


def sublane_iota(rows, lanes=LANES):
    return lax.broadcasted_iota(i32, (rows, lanes), 0)


def as_column(row):
    parts = [
        jnp.broadcast_to(row[:, i * LANES : (i + 1) * LANES], (LANES, LANES)).T
        for i in range(row.shape[1] // LANES)
    ]
    return parts[0] if len(parts) == 1 else jnp.concatenate(parts, axis=0)


class Layout:
    def __init__(self, peers, tokens, heads):
        self.peers, self.tokens, self.heads = peers, tokens, heads
        self.stripe = min(16, peers)
        self.runs = peers // self.stripe
        self.per_dev = CLUSTER // self.stripe
        self.rows_peer = tokens // peers
        self.half_rows = self.rows_peer // 2
        self.pairs = self.half_rows // self.per_dev
        self.packed = tokens // 2
        self.clusters = peers * tokens // CLUSTER
        self.data_rows = 9 * self.half_rows
        self.direct = self.half_rows == LANES
        self.arrays = peers if self.direct else 1

    def peer(self, me, s):
        return (me ^ s) if self.direct else s

    def shapes(self, rows, dtype=bf16):
        lead = () if self.direct else (self.peers,)
        return [jax.ShapeDtypeStruct(lead + (rows, LANES), dtype)] * self.arrays

    def specs(self, rows, at):
        if self.direct:
            return [pl.BlockSpec((rows, LANES), lambda *g: (at(*g), 0))] * self.arrays
        return [pl.BlockSpec((self.peers, rows, LANES), lambda *g: (0, at(*g), 0))]

    def view(self, refs, s):
        return refs[s] if self.direct else refs[0].at[s]


def only(at):
    return lambda *g: at


def place_kernel(lay, perm_ref, code_ref):
    groups = lay.clusters
    shift = CLUSTER.bit_length() - 1
    blocks = lay.tokens // LANES
    before = sublane_iota(LANES, 2 * LANES)
    after = lane_iota(LANES, 2 * LANES)
    ahead_of = jnp.where((before < after) | (after >= LANES), 1.0, 0.0).astype(bf16)

    def members(h, b):
        row = lax.shift_right_logical(perm_ref[h : h + 1, b * LANES : (b + 1) * LANES], shift)
        return jnp.broadcast_to(row, (groups, LANES)) == sublane_iota(groups)

    for h in range(lay.heads):
        if lay.runs == 1:
            carry = (sublane_iota(groups) * lay.per_dev).astype(f32)
        else:
            counts = jnp.zeros((groups, LANES), f32)
            for b in range(blocks):
                member = jnp.where(members(h, b), 1.0, 0.0).astype(bf16)
                counts = counts + nn(member, ahead_of)[:, LANES:]
            lower = jnp.where(
                sublane_iota(groups, groups) > lane_iota(groups, groups), 1.0, 0.0
            ).astype(bf16)
            carry = nn(lower, counts.astype(bf16))
        for b in range(blocks):
            member = members(h, b)
            found = nn(jnp.where(member, 1.0, 0.0).astype(bf16), ahead_of)
            rank = jnp.sum(jnp.where(member, found[:, :LANES] + carry, 0.0), axis=0, keepdims=True)
            carry = carry + found[:, LANES:]
            rank = rank.astype(i32)
            peer = lax.shift_right_logical(rank, lay.rows_peer.bit_length() - 1)
            rest = rank & (lay.rows_peer - 1)
            half = lax.shift_right_logical(rest, lay.half_rows.bit_length() - 1)
            packed = peer * lay.half_rows + (rest & (lay.half_rows - 1))
            at = slice(b * LANES, (b + 1) * LANES)
            code_ref[h, 0:1, at] = packed
            code_ref[h, 1:2, at] = half


def place_tokens(lay, perm):
    return pl.pallas_call(
        partial(place_kernel, lay),
        out_shape=jax.ShapeDtypeStruct((lay.heads, 8, lay.tokens), i32),
        name="place_tokens",
        cost_estimate=QUICK,
    )(perm)


def one_hot(equal):
    return jnp.where(equal, 1.0, 0.0).astype(bf16)


def scatter_matrix(lay, me, packed, s, blocks):
    rows = blocks * lay.half_rows
    if lay.direct:
        parts = [
            one_hot(
                jnp.broadcast_to(packed, (lay.half_rows, lay.tokens))
                == sublane_iota(lay.half_rows, lay.tokens) + lay.peer(me, s + i) * lay.half_rows
            )
            for i in range(blocks)
        ]
        return jnp.concatenate(parts, axis=0)
    wanted = sublane_iota(rows, lay.tokens) + s * lay.half_rows
    return one_hot(jnp.broadcast_to(packed, (rows, lay.tokens)) == wanted)


def gather_matrix(lay, me, column):
    lane = lane_iota(column.shape[0])
    parts = [
        one_hot(column == lane + lay.peer(me, k) * LANES) for k in range(lay.packed // LANES)
    ]
    return jnp.concatenate(parts, axis=1)


def block_rows(lay, refs, first):
    at = slice(first, first + lay.half_rows)
    if lay.direct:
        return jnp.concatenate([refs[s][at, :] for s in range(lay.peers)], axis=0)
    return refs[0][:, at, :].astype(f32).reshape(lay.packed, LANES).astype(bf16)


def put_blocks(lay, refs, s, blocks, first, rows):
    at = slice(first, first + lay.half_rows) if isinstance(first, int) else pl.ds(first, lay.half_rows)
    if lay.direct:
        for i in range(blocks):
            refs[s + i][at, :] = rows[i * LANES : (i + 1) * LANES].astype(bf16)
    else:
        rows = rows.astype(f32).reshape(blocks, lay.half_rows, LANES).astype(bf16)
        refs[0][s : s + blocks, at, :] = rows


def project_kernel(lay, steps, place_ref, x_ref, w_ref, bias_ref, code_ref, pad_ref, *rest):
    outs = rest[: lay.arrays]
    rows_ref, flag_ref = rest[lay.arrays :]
    step = pl.program_id(0)
    me = place_ref[0]
    width = 4 * LANES

    @pl.when(step < steps)
    def _():
        at = pl.ds(pl.multiple_of(step * 256, 256), 256)
        values = nn(x_ref[...], w_ref[...]) + bias_ref[0:1, :]
        low = lane_iota(256) < HEAD_DIM
        lane_half = jnp.where(low, 0, 1)
        live = as_column(pad_ref[0:1, at])
        tiles = [values[:, i * LANES : (i + 1) * LANES] for i in range(values.shape[1] // LANES)]
        turned = [pltpu.roll(tile, HEAD_DIM, 1) for tile in tiles]
        for h in range(lay.heads):
            half = as_column(code_ref[h, 1:2, at])
            keep = half == lane_half
            v, side = lay.heads + h // 2, h % 2
            planes = (
                jnp.where(low, tiles[h], turned[h]),
                jnp.where(low, turned[h], tiles[h]),
                jnp.where(low, tiles[v], turned[v]) if side == 0 else jnp.where(low, turned[v], tiles[v]),
            )
            for x, plane in enumerate(planes):
                rows_ref[h, at, x * LANES : (x + 1) * LANES] = jnp.where(keep, plane, 0.0).astype(bf16)
            flags = jnp.where((lane_iota(256) == half) & (live == 1), 1.0, 0.0)
            rows_ref[h, at, 3 * LANES :] = flags.astype(bf16)

    count = 4 if lay.direct else 32
    for h in range(lay.heads):

        @pl.when(step == steps + h)
        def _():
            for s in range(0, lay.peers, count):
                chosen = scatter_matrix(lay, me, code_ref[h, 0:1, :], s, count)
                moved = nn(chosen, rows_ref[h])
                for x in range(3):
                    put_blocks(
                        lay, outs, s, count, (h * 3 + x) * lay.half_rows,
                        moved[:, x * LANES : (x + 1) * LANES],
                    )
                for i in range(count * lay.half_rows // LANES):
                    at = slice(s * lay.half_rows + i * LANES, s * lay.half_rows + (i + 1) * LANES)
                    flag_ref[h, :, at] = moved[i * LANES : (i + 1) * LANES, 3 * LANES :].T[:8]

    @pl.when(step == steps + lay.heads - 1)
    def _():
        for s in range(lay.peers):
            at = slice(s * lay.half_rows, (s + 1) * lay.half_rows)
            rows = [flag_ref[k, 0:2, at] for k in range(lay.heads)]
            block = jnp.concatenate(rows + [jnp.zeros((16 - 2 * lay.heads, lay.half_rows), f32)], axis=0)
            if lay.half_rows < LANES:
                block = jnp.concatenate(
                    [block, jnp.zeros((16, LANES - lay.half_rows), f32)], axis=1
                )
            lay.view(outs, s)[lay.data_rows : lay.data_rows + 16, :] = block.astype(bf16)


def project_rows(lay, places, x, weights, bias, code, pad):
    width = weights.shape[1]
    steps = lay.tokens // 256
    spec = pltpu.PrefetchScalarGridSpec(
        num_scalar_prefetch=1,
        grid=(steps + lay.heads,),
        in_specs=[
            pl.BlockSpec((256, D), lambda s, _: (jnp.minimum(s, steps - 1), 0)),
            pl.BlockSpec((D, width), lambda s, _: (0, 0)),
            pl.BlockSpec((8, width), lambda s, _: (0, 0)),
            pl.BlockSpec((lay.heads, 8, lay.tokens), lambda s, _: (0, 0, 0)),
            pl.BlockSpec((1, lay.tokens), lambda s, _: (0, 0)),
        ],
        out_specs=lay.specs(lay.data_rows + 16, only(0)),
        scratch_shapes=[
            pltpu.VMEM((lay.heads, lay.tokens, 4 * LANES), bf16),
            pltpu.VMEM((lay.heads, 8, lay.packed), f32),
        ],
    )
    return pl.pallas_call(
        partial(project_kernel, lay, steps),
        grid_spec=spec,
        out_shape=lay.shapes(lay.data_rows + 16),
        compiler_params=pltpu.CompilerParams(vmem_limit_bytes=VMEM),
        name="project_rows",
        cost_estimate=QUICK,
    )(places, x, weights, bias, code, pad)


def pair_rows(lay, refs, first, run, p):
    at = slice(first + p * lay.per_dev, first + (p + 1) * lay.per_dev)
    if lay.direct:
        return jnp.concatenate([refs[s][at, :] for s in range(lay.stripe)], axis=0)
    block = refs[0][run * lay.stripe : (run + 1) * lay.stripe, first : first + lay.half_rows, :]
    block = block.astype(f32)[:, p * lay.per_dev : (p + 1) * lay.per_dev, :]
    return block.reshape(CLUSTER, LANES).astype(bf16)


def put_pair(lay, refs, first, run, p, rows):
    at = slice(first + p * lay.per_dev, first + (p + 1) * lay.per_dev)
    for s in range(lay.stripe):
        part = rows[s * lay.per_dev : (s + 1) * lay.per_dev]
        lay.view(refs, run * lay.stripe + s)[at, :] = part.astype(bf16)


def live_columns(lay, flags, h):
    pick = one_hot(sublane_iota(16, 2 * LANES) == 2 * h + lane_iota(16, 2 * LANES) // LANES)
    return [tn(lay.view(flags, s)[...], pick) for s in range(lay.peers)]


def allowed_pair(lay, columns, run, p):
    at = slice(p * lay.per_dev, (p + 1) * lay.per_dev)
    live = jnp.concatenate([columns[run * lay.stripe + s][at] for s in range(lay.stripe)], axis=0)
    live = jnp.concatenate([live[:, :LANES], live[:, LANES:]], axis=0)
    same = sublane_iota(2 * CLUSTER) % CLUSTER == lane_iota(2 * CLUSTER)
    return (live > 0.5) | same


def stack_halves(rows):
    low = lane_iota(rows.shape[0], rows.shape[1]) < HEAD_DIM
    zero = jnp.zeros_like(rows)
    return jnp.concatenate([jnp.where(low, rows, zero), jnp.where(low, zero, rows)], axis=0)


def each_half(fold, rows):
    one, two = (
        jnp.broadcast_to(fold(part, axis=0, keepdims=True), part.shape)
        for part in (rows[:CLUSTER], rows[CLUSTER:])
    )
    return jnp.concatenate([one, two], axis=0)


def inverse_sum(rows, axis, keepdims):
    return 1.0 / jnp.sum(rows, axis=axis, keepdims=keepdims)


def soft_weights(queries, keys, allowed):
    scores = jnp.where(allowed, nt(keys, queries) * SCALE, MASKED)
    grown = jnp.exp(scores - each_half(jnp.max, scores))
    return grown * each_half(inverse_sum, grown)


def attend_kernel(lay, *refs):
    rows, flags, outs = (refs[i * lay.arrays : (i + 1) * lay.arrays] for i in range(3))
    live = live_columns(lay, flags, pl.program_id(0))
    for run in range(lay.runs):
        for p in range(lay.pairs):
            q, k, v = (pair_rows(lay, rows, x * lay.half_rows, run, p) for x in range(3))
            soft = soft_weights(q, stack_halves(k), allowed_pair(lay, live, run, p))
            put_pair(lay, outs, 0, run, p, tn(soft.astype(bf16), stack_halves(v)))


def attend(lay, arrived):
    head = lambda h: h
    return pl.pallas_call(
        partial(attend_kernel, lay),
        grid=(lay.heads,),
        in_specs=lay.specs(3 * lay.half_rows, head) + lay.specs(16, only(lay.data_rows // 16)),
        out_specs=lay.specs(lay.half_rows, head),
        out_shape=lay.shapes(lay.heads * lay.half_rows),
        name="attend",
        cost_estimate=QUICK,
    )(*arrived, *arrived)


def attend_back_kernel(lay, *refs):
    rows, flags, grads, outs = (refs[i * lay.arrays : (i + 1) * lay.arrays] for i in range(4))
    sum_ref = refs[-1]
    live = live_columns(lay, flags, pl.program_id(0))
    low = lane_iota(CLUSTER) < HEAD_DIM
    sums = [jnp.zeros((1, LANES), f32)] * 2
    for run in range(lay.runs):
        for p in range(lay.pairs):
            q, k, v = (pair_rows(lay, rows, x * lay.half_rows, run, p) for x in range(3))
            g = pair_rows(lay, grads, 0, run, p)
            keys = stack_halves(k)
            soft = soft_weights(q, keys, allowed_pair(lay, live, run, p))
            grad_soft = nt(stack_halves(v), g)
            delta = each_half(jnp.sum, soft * grad_soft)
            grad = (soft * (grad_soft - delta)).astype(bf16)
            grad_q = (tn(grad, keys) * SCALE).astype(bf16)
            part = nn(grad, q)
            grad_k = (jnp.where(low, part[:CLUSTER], part[CLUSTER:]) * SCALE).astype(bf16)
            part = nn(soft.astype(bf16), g)
            grad_v = jnp.where(low, part[:CLUSTER], part[CLUSTER:]).astype(bf16)
            for x, part in enumerate((grad_q, grad_k, grad_v)):
                put_pair(lay, outs, x * lay.half_rows, run, p, part)
            sums[0] = sums[0] + jnp.sum(grad_q.astype(f32), axis=0, keepdims=True)
            sums[1] = sums[1] + jnp.sum(grad_v.astype(f32), axis=0, keepdims=True)
    sum_ref[0] = jnp.concatenate(sums + [jnp.zeros((6, LANES), f32)], axis=0)


def attend_back(lay, arrived, grads):
    head = lambda h: h
    three = lay.specs(3 * lay.half_rows, head)
    out = pl.pallas_call(
        partial(attend_back_kernel, lay),
        grid=(lay.heads,),
        in_specs=three
        + lay.specs(16, only(lay.data_rows // 16))
        + lay.specs(lay.half_rows, head),
        out_specs=three + [pl.BlockSpec((1, 8, LANES), lambda h: (h, 0, 0))],
        out_shape=lay.shapes(lay.data_rows)
        + [jax.ShapeDtypeStruct((lay.heads, 8, LANES), f32)],
        name="attend_back",
        cost_estimate=QUICK,
    )(*arrived, *arrived, *grads)
    return out[:-1], out[-1]


def side_rows(quarter, side):
    return pl.ds(pl.multiple_of(quarter * 512 + side * 256, 256), 256)


def unsort_kernel(lay, place_ref, *refs):
    rows_refs, code_ref, outs = refs[: lay.arrays], refs[lay.arrays], refs[lay.arrays + 1 :]
    rows = block_rows(lay, rows_refs, 0)
    low = lane_iota(256) < HEAD_DIM
    me, place = place_ref[0], place_ref[1]

    for t in range(4):
        sides = []
        for side in range(2):
            at = side_rows(place ^ t, side)
            column = as_column(code_ref[0, 0:1, at])
            half = as_column(code_ref[0, 1:2, at])
            found = nn(gather_matrix(lay, me, column), rows)
            sides.append(jnp.where(half == side, found, pltpu.roll(found, HEAD_DIM, 1)))
        outs[t][...] = jnp.where(low, sides[0], sides[1]).astype(bf16)


def unsort_rows(lay, places, returned, code):
    spec = pltpu.PrefetchScalarGridSpec(
        num_scalar_prefetch=1,
        grid=(lay.heads,),
        in_specs=lay.specs(lay.half_rows, lambda h, _: h)
        + [pl.BlockSpec((1, 8, lay.tokens), lambda h, _: (h, 0, 0))],
        out_specs=[pl.BlockSpec((256, LANES), lambda h, _: (0, h))] * 4,
    )
    return pl.pallas_call(
        partial(unsort_kernel, lay),
        grid_spec=spec,
        out_shape=[jax.ShapeDtypeStruct((256, lay.heads * LANES), bf16)] * 4,
        name="unsort_rows",
        cost_estimate=QUICK,
    )(places, *returned, code)


def sort_kernel(lay, place_ref, *refs):
    grads, code_ref, outs, rows_ref = refs[:4], refs[4], refs[5:-1], refs[-1]
    low = lane_iota(256) < HEAD_DIM
    lane_half = jnp.where(low, 0, 1)
    me, place = place_ref[0], place_ref[1]

    for t in range(4):
        block = grads[t][...].astype(f32)
        turned = pltpu.roll(block, HEAD_DIM, 1)
        for side in range(2):
            at = side_rows(place ^ t, side)
            half = as_column(code_ref[0, 1:2, at])
            both = jnp.where(low, block, turned) if side == 0 else jnp.where(low, turned, block)
            rows_ref[at, :] = jnp.where(half == lane_half, both, 0.0).astype(bf16)

    count = 4 if lay.direct else 32
    for s in range(0, lay.peers, count):
        chosen = scatter_matrix(lay, me, code_ref[0, 0:1, :], s, count)
        put_blocks(lay, outs, s, count, 0, nn(chosen, rows_ref[...]))


def sort_rows(lay, places, grads, code):
    spec = pltpu.PrefetchScalarGridSpec(
        num_scalar_prefetch=1,
        grid=(lay.heads,),
        in_specs=[pl.BlockSpec((256, LANES), lambda h, _: (0, h))] * 4
        + [pl.BlockSpec((1, 8, lay.tokens), lambda h, _: (h, 0, 0))],
        out_specs=lay.specs(lay.half_rows, lambda h, _: h),
        scratch_shapes=[pltpu.VMEM((lay.tokens, LANES), bf16)],
    )
    return pl.pallas_call(
        partial(sort_kernel, lay),
        grid_spec=spec,
        out_shape=lay.shapes(lay.heads * lay.half_rows),
        name="sort_rows",
        cost_estimate=QUICK,
    )(places, *grads, code)


def pack_kernel(
    query_ref, key_ref, value_ref, output_ref, inner_ref, outer_ref,
    bias_ref, gain_ref, shift_ref, inner_bias_ref, piece_ref, shard_ref, outer_out_ref,
):
    depth, width = query_ref.shape
    heads = width // HEAD_DIM
    query, key, value = (ref[...].astype(f32) for ref in (query_ref, key_ref, value_ref))
    cut = [slice(h * HEAD_DIM, (h + 1) * HEAD_DIM) for h in range(heads)]
    columns = [part for at in cut for part in (query[:, at], key[:, at])] + [value]
    have = 3 * width
    fill = piece_ref.shape[1] - have
    if fill:
        columns.append(jnp.zeros((depth, fill), f32))
    piece_ref[:depth, :] = jnp.concatenate(columns, axis=1).astype(bf16)
    inner_bias = inner_bias_ref[...].astype(f32)
    vectors = jnp.concatenate(
        [ref[...].astype(f32) for ref in (bias_ref, gain_ref, shift_ref)]
        + [inner_bias[:, i * depth : (i + 1) * depth] for i in range(4)]
        + [jnp.zeros((4, depth), f32)],
        axis=0,
    )
    vectors = jnp.concatenate([vectors, jnp.zeros((16, piece_ref.shape[1] - depth), f32)], axis=1)
    piece_ref[depth:, :] = vectors.astype(bf16)
    shard_ref[:, :D] = inner_ref[...]
    outer_out_ref[...] = outer_ref[...]
    turned = output_ref[...].astype(f32).T
    shard_ref[:, D:] = jnp.concatenate(
        [turned[:, at] for at in cut for _ in range(2)], axis=1
    ).astype(bf16)


def pack_weights(*arrays):
    depth, width = arrays[0].shape
    columns = -(-3 * width // LANES) * LANES
    return pl.pallas_call(
        pack_kernel,
        out_shape=[
            jax.ShapeDtypeStruct((depth + 16, columns), bf16),
            jax.ShapeDtypeStruct((depth, D + 2 * width), bf16),
            jax.ShapeDtypeStruct((depth, D), bf16),
        ],
        name="pack_weights",
        cost_estimate=QUICK,
    )(*arrays)


def assemble_kernel(lay, place_ref, *refs):
    pieces, (weight_ref, bias_ref, par_ref, part_ref) = refs[: lay.peers], refs[lay.peers :]
    me, place = place_ref[0], place_ref[1]
    depth = D // lay.peers
    for s in range(lay.peers):
        d = me ^ s
        weight_ref[pl.ds(pl.multiple_of(d * depth, 16), depth), :] = pieces[s][:depth, :]
        part_ref[d] = pieces[s][depth:, :LANES].astype(f32)

    def whole(row, rows=1, peers=range(lay.peers)):
        return jnp.concatenate(
            [part_ref[d, row + i : row + i + 1, :depth] for d in peers for i in range(rows)], axis=1
        )

    vectors = [whole(r) for r in range(8)]
    each = lay.peers // 4
    vectors += [whole(8, 4, range(j * each, (j + 1) * each)) for j in range(4)]
    par_ref[...] = jnp.concatenate(vectors + [jnp.zeros((4, D), f32)], axis=0)
    width = lay.heads * HEAD_DIM

    def own(vector):
        out = vector[:, :width]
        for p in range(1, D // width):
            out = jnp.where(place == p, vector[:, p * width : (p + 1) * width], out)
        return out

    query = own(vectors[0])
    zero = jnp.zeros((1, HEAD_DIM), f32)
    columns = [
        part for h in range(lay.heads) for part in (query[:, h * HEAD_DIM : (h + 1) * HEAD_DIM], zero)
    ] + [own(vectors[1])]
    fill = bias_ref.shape[1] - 3 * width
    if fill:
        columns.append(jnp.zeros((1, fill), f32))
    bias_ref[...] = jnp.broadcast_to(jnp.concatenate(columns, axis=1), bias_ref.shape)


def assemble_weights(lay, places, pieces):
    columns = pieces[0].shape[1]
    vmem = pl.BlockSpec(memory_space=pltpu.VMEM)
    return pl.pallas_call(
        partial(assemble_kernel, lay),
        in_specs=[pl.BlockSpec(memory_space=pltpu.SMEM)] + [vmem] * lay.peers,
        out_specs=[vmem] * 3,
        out_shape=[
            jax.ShapeDtypeStruct((D, columns), bf16),
            jax.ShapeDtypeStruct((8, columns), f32),
            jax.ShapeDtypeStruct((16, D), f32),
        ],
        scratch_shapes=[pltpu.VMEM((lay.peers, 16, LANES), f32)],
        name="assemble_weights",
        cost_estimate=QUICK,
    )(places, *pieces)


def mean_rows(v):
    return jnp.sum(v, axis=1, keepdims=True) * (1.0 / D)


def norm_forward(rows):
    centred = rows - mean_rows(rows)
    inv = lax.rsqrt(mean_rows(centred * centred) + EPSILON)
    return centred * inv, inv


def norm_backward(scaled, normed, inv):
    return inv * (scaled - mean_rows(scaled) - normed * mean_rows(scaled * normed))


def middle_kernel(
    place_ref,
    att0,
    att1,
    att2,
    att3,
    hidden_ref,
    cot_ref,
    par_ref,
    w0,
    w1,
    w2,
    w3,
    v0,
    v1,
    v2,
    v3,
    out_ref,
    act_ref,
    pre_ref,
    low_ref,
    ffn_grad_ref,
    branch_grad_ref,
    h1_ref,
    grad0,
    grad1,
    grad2,
    grad3,
    vec_ref,
    first_ref,
    normed_ref,
    inv_ref,
    slope_ref,
    sum_ref,
    h2_ref,
    weight_ref,
    sems,
):
    step = pl.program_id(0)
    place = place_ref[1]
    project = slice(2 * D, None)

    def fetch(t, part):
        width = att0.shape[1]
        source = (w0, w1, w2, w3)[t].at[:, D:], (w0, w1, w2, w3)[t].at[:, :D], (v0, v1, v2, v3)[t]
        target = pl.ds(2 * D, width), pl.ds(0, D), pl.ds(D, D)
        return pltpu.make_async_copy(
            source[part], weight_ref.at[t, :, target[part]], sems.at[part, t]
        )

    for t in range(4):

        @pl.when(step == t + 1)
        def _():
            fetch(t, 1).wait()
            fetch(t, 2).wait()

    @pl.when(step == 0)
    def _():
        for t in range(4):
            fetch(t, 0).start()
        for t in range(4):
            fetch(t, 1).start()
            fetch(t, 2).start()
        for t in range(4):
            fetch(t, 0).wait()
        vec_ref[...] = jnp.zeros_like(vec_ref)
        for side in range(2):
            branch = jnp.zeros((256, D), f32)
            for t, att_ref in enumerate((att0, att1, att2, att3)):
                att = att_ref[...]
                lane = lane_iota(256, att.shape[1]) % LANES
                own = (lane < HEAD_DIM) if side == 0 else (lane >= HEAD_DIM)
                branch = branch + nt(jnp.where(own, att, jnp.zeros_like(att)), weight_ref[t, :, project])
            at = slice(side * 256, side * 256 + 256)
            rows = hidden_ref[at, :].astype(f32) + (branch + par_ref[2:3, :])
            normed, inv = norm_forward(rows)
            first = normed * par_ref[4:5, :] + par_ref[6:7, :]
            first_ref[at, :] = first
            normed_ref[at, :] = normed
            inv_ref[at, :] = jnp.broadcast_to(inv, (256, LANES))
            low_ref[at, :] = first.astype(bf16)
        sum_ref[...] = jnp.zeros_like(sum_ref)

    @pl.when((step >= 1) & (step <= 4))
    def _():
        j = step - 1
        for side in range(2):
            at = slice(side * 256, side * 256 + 256)
            pre = nn(low_ref[at, :], weight_ref[j, :, :D]) + par_ref[pl.ds(8 + (place ^ j), 1), :]
            cdf = 0.5 * (1.0 + lax.erf(pre * (1.0 / math.sqrt(2.0))))
            slope_ref[j, at, :] = cdf + pre * jnp.exp(-0.5 * pre * pre) * (1.0 / math.sqrt(2.0 * math.pi))
            act = (pre * cdf).astype(bf16)
            act_ref[at, :] = act
            sum_ref[at, :] += nt(act, weight_ref[j, :, D : 2 * D])

    @pl.when(step == 4)
    def _():
        for side in range(4):
            at = slice(side * 128, side * 128 + 128)
            rows = first_ref[at, :] + (sum_ref[at, :] + par_ref[3:4, :])
            normed, inv = norm_forward(rows)
            out_ref[at, :] = (normed * par_ref[5:6, :] + par_ref[7:8, :]).astype(bf16)
            cot = cot_ref[at, :].astype(f32)
            grad = norm_backward(cot * par_ref[5:6, :], normed, inv)
            grad_low = grad.astype(bf16)
            h2_ref[at, :] = grad
            ffn_grad_ref[at, :] = grad_low
            vec_ref[3:4, :] += jnp.sum(grad_low.astype(f32), axis=0, keepdims=True)
            vec_ref[5:6, :] += jnp.sum(cot * normed, axis=0, keepdims=True)
            vec_ref[7:8, :] += jnp.sum(cot, axis=0, keepdims=True)
        sum_ref[...] = jnp.zeros_like(sum_ref)

    @pl.when(step >= 5)
    def _():
        j = 8 - step
        total = jnp.zeros((1, D), f32)
        for side in range(2):
            at = slice(side * 256, side * 256 + 256)
            grad_act = nn(ffn_grad_ref[at, :], weight_ref[j, :, D : 2 * D])
            grad_pre = (grad_act * slope_ref[j, at, :]).astype(bf16)
            pre_ref[at, :] = grad_pre
            total = total + jnp.sum(grad_pre.astype(f32), axis=0, keepdims=True)
            sum_ref[at, :] += nt(grad_pre, weight_ref[j, :, :D])
        vec_ref[pl.ds(8 + (place ^ j), 1), :] = total

    @pl.when(step == 8)
    def _():
        for side in range(4):
            at = slice(side * 128, side * 128 + 128)
            grad_first = h2_ref[at, :] + sum_ref[at, :]
            normed = normed_ref[at, :]
            grad = norm_backward(grad_first * par_ref[4:5, :], normed, inv_ref[at, 0:1])
            grad_low = grad.astype(bf16)
            h1_ref[at, :] = grad
            branch_grad_ref[at, :] = grad_low
            vec_ref[2:3, :] += jnp.sum(grad_low.astype(f32), axis=0, keepdims=True)
            vec_ref[4:5, :] += jnp.sum(grad_first * normed, axis=0, keepdims=True)
            vec_ref[6:7, :] += jnp.sum(grad_first, axis=0, keepdims=True)
        for t, grad_ref in enumerate((grad0, grad1, grad2, grad3)):
            both = [
                nn(branch_grad_ref[s * 256 : s * 256 + 256, :], weight_ref[t, :, project])
                for s in range(2)
            ]
            lane = lane_iota(256, both[0].shape[1]) % LANES
            grad_ref[...] = jnp.where(lane < HEAD_DIM, both[0], both[1]).astype(bf16)


def middle(places, att, hidden, cotangent, params, weights):
    width = att[0].shape[1]
    rows = 512

    def up(s, q):
        return (0, jnp.clip(s - 1, 0, 3))

    def down(s, q):
        return (0, jnp.clip(8 - s, 0, 3))

    def whole(rank):
        return lambda s, q: (0,) * rank

    square = pl.BlockSpec((rows, D), whole(2))
    exchanged = pl.BlockSpec((256, width), whole(2))
    spec = pltpu.PrefetchScalarGridSpec(
        num_scalar_prefetch=1,
        grid=(9,),
        in_specs=[exchanged] * 4
        + [
            pl.BlockSpec((rows, D), lambda s, q: (q[1], 0)),
            pl.BlockSpec((rows, D), lambda s, q: (q[1], 0)),
            pl.BlockSpec((16, D), whole(2)),
        ]
        + [pl.BlockSpec(memory_space=pl.ANY)] * 8,
        out_specs=[
            square,
            pl.BlockSpec((rows, D), up),
            pl.BlockSpec((rows, D), down),
            square,
            square,
            square,
            square,
        ]
        + [exchanged] * 4
        + [pl.BlockSpec((16, D), whole(2))],
        scratch_shapes=[
            pltpu.VMEM((rows, D), f32),
            pltpu.VMEM((rows, D), f32),
            pltpu.VMEM((rows, LANES), f32),
            pltpu.VMEM((4, rows, D), f32),
            pltpu.VMEM((rows, D), f32),
            pltpu.VMEM((rows, D), f32),
            pltpu.VMEM((4, D, 2 * D + width), bf16),
            pltpu.SemaphoreType.DMA((3, 4)),
        ],
    )
    out = pl.pallas_call(
        middle_kernel,
        grid_spec=spec,
        out_shape=[
            jax.ShapeDtypeStruct((rows, D), bf16),
            jax.ShapeDtypeStruct((rows, FF), bf16),
            jax.ShapeDtypeStruct((rows, FF), bf16),
            jax.ShapeDtypeStruct((rows, D), bf16),
            jax.ShapeDtypeStruct((rows, D), bf16),
            jax.ShapeDtypeStruct((rows, D), bf16),
            jax.ShapeDtypeStruct((rows, D), f32),
        ]
        + [jax.ShapeDtypeStruct((256, width), bf16)] * 4
        + [jax.ShapeDtypeStruct((16, D), f32)],
        compiler_params=pltpu.CompilerParams(vmem_limit_bytes=VMEM),
        name="middle",
        cost_estimate=QUICK,
    )(places, *att, hidden, cotangent, params, *weights)
    return out[:7], out[7:11], out[11]


def weight_grad_kernel(place_ref, act_ref, pre_ref, low_ref, ffn_ref, branch_ref, *refs):
    att_refs, out_ref = refs[:-1], refs[-1]
    out_ref[:, :D] = tn(low_ref[...], pre_ref[...]).astype(bf16)
    out_ref[:, D : 2 * D] = tn(ffn_ref[...], act_ref[...]).astype(bf16)
    for t in range(4):

        @pl.when(pl.program_id(0) == t)
        def _():
            att = att_refs[t][...]
            low = lane_iota(256, att.shape[1]) % LANES < HEAD_DIM
            zero = jnp.zeros_like(att)
            part = tn(branch_ref[:256, :], jnp.where(low, att, zero))
            part = part + tn(branch_ref[256:, :], jnp.where(low, zero, att))
            out_ref[:, 2 * D :] = part.astype(bf16)


def weight_grads(places, saved, att):
    act, pre, low, ffn_grad, branch_grad = saved
    rows = act.shape[0]
    width = att[0].shape[1]
    total = 2 * D + width
    whole = pl.BlockSpec((rows, D), lambda t, q: (0, 0))
    part = pl.BlockSpec((rows, D), lambda t, q: (0, t))
    spec = pltpu.PrefetchScalarGridSpec(
        num_scalar_prefetch=1,
        grid=(4,),
        in_specs=[part] * 2
        + [whole] * 3
        + [pl.BlockSpec((256, width), lambda t, q: (0, 0))] * 4,
        out_specs=pl.BlockSpec((D, total), lambda t, q: (q[1] ^ t, 0)),
    )
    return pl.pallas_call(
        weight_grad_kernel,
        grid_spec=spec,
        out_shape=jax.ShapeDtypeStruct((4 * D, total), bf16),
        compiler_params=pltpu.CompilerParams(vmem_limit_bytes=VMEM),
        name="weight_grads",
        cost_estimate=QUICK,
    )(places, act, pre, low, ffn_grad, branch_grad, *att)


def token_chunk(lay, g, c, place):
    core = place % 2
    half = jnp.where(c < 2, 1 - core, core)
    return half * (lay.tokens // 512) + g * 2 + c % 2


def collect_kernel(lay, g, place_ref, *refs):
    rows_refs = refs[: lay.arrays]
    code_ref, w_ref, h1_ref, other_ref, mine_ref, dense_ref = refs[lay.arrays :]
    chunk = pl.program_id(0)
    me, place = place_ref[0], place_ref[1]
    low = lane_iota(256) < HEAD_DIM
    firsts, seconds = [], []
    for h in range(lay.heads):
        column = as_column(code_ref[h, 0:1, :])
        half = as_column(code_ref[h, 1:2, :])
        planes = [block_rows(lay, rows_refs, (h * 3 + x) * lay.half_rows) for x in range(3)]
        found = nn(gather_matrix(lay, me, column), jnp.concatenate(planes, axis=1))
        one, two = [], []
        for x in range(3):
            part = found[:, x * LANES : (x + 1) * LANES]
            turned = pltpu.roll(part, HEAD_DIM, 1)
            one.append(jnp.where(half == 0, part, turned))
            two.append(jnp.where(half == 1, part, turned))
        firsts.append(one)
        seconds.append(two)
    tiles = [jnp.where(low, firsts[h][0], seconds[h][1]) for h in range(lay.heads)]
    for h in range(0, lay.heads, 2):
        right = seconds[h + 1][2] if h + 1 < lay.heads else jnp.zeros((256, LANES), f32)
        tiles.append(jnp.where(low, firsts[h][2], right))
    dense = jnp.concatenate(tiles, axis=1).astype(bf16)
    dense_ref[...] = dense
    part = nt(dense, w_ref[...])
    at = token_chunk(lay, g, chunk, place)
    own = (at // 2 == place).astype(f32)
    part = part + own * h1_ref[pl.ds(pl.multiple_of(at % 2 * 256, 256), 256), :]

    @pl.when(chunk < 2)
    def _():
        other_ref[...] = part.astype(bf16)

    @pl.when(chunk >= 2)
    def _():
        mine_ref[...] = part.astype(bf16)


def collect(lay, g, places, returned, code, weights, grad_h1):
    width = weights.shape[1]
    spec = pltpu.PrefetchScalarGridSpec(
        num_scalar_prefetch=1,
        grid=(4,),
        in_specs=lay.specs(lay.data_rows, only(0))
        + [
            pl.BlockSpec((lay.heads, 8, 256), lambda c, q: (0, 0, token_chunk(lay, g, c, q[1]))),
            pl.BlockSpec((D, width), lambda c, q: (0, 0)),
            pl.BlockSpec((512, D), lambda c, q: (0, 0)),
        ],
        out_specs=[
            pl.BlockSpec((256, D), lambda c, q: (jnp.minimum(c, 1), 0)),
            pl.BlockSpec((256, D), lambda c, q: (jnp.maximum(c - 2, 0), 0)),
            pl.BlockSpec((256, width), lambda c, q: (c, 0)),
        ],
    )
    return pl.pallas_call(
        partial(collect_kernel, lay, g),
        grid_spec=spec,
        out_shape=[
            jax.ShapeDtypeStruct((512, D), bf16),
            jax.ShapeDtypeStruct((512, D), bf16),
            jax.ShapeDtypeStruct((1024, width), bf16),
        ],
        compiler_params=pltpu.CompilerParams(vmem_limit_bytes=VMEM),
        name="collect",
        cost_estimate=QUICK,
    )(places, *returned, code, weights, grad_h1)


def head_grad_kernel(lay, place_ref, x_ref, dense0_ref, dense1_ref, vec_ref, *refs):
    outs, total_ref = refs[: lay.arrays], refs[-1]
    step = pl.program_id(0)

    @pl.when(step == 0)
    def _():
        total_ref[...] = tn(x_ref[...], dense0_ref[...])

    @pl.when((step > 0) & (step < 4))
    def _():
        total_ref[...] += tn(x_ref[...], dense0_ref[...])

    @pl.when(step >= 4)
    def _():
        total_ref[...] += tn(x_ref[...], dense1_ref[...])

    @pl.when(step == 7)
    def _():
        depth = D // lay.peers
        if not lay.direct:
            outs[0][...] = total_ref[...].astype(bf16)
            return
        for s in range(lay.peers):
            d = place_ref[0] ^ s
            outs[s][:depth, :] = total_ref[pl.ds(pl.multiple_of(d * depth, 8), depth), :].astype(bf16)
            vector = vec_ref[d]
            high = vector.astype(bf16).astype(f32)
            width = total_ref.shape[1]
            outs[s][depth:, :] = jnp.concatenate(
                [high, vector - high, jnp.zeros((16, width - 2 * LANES), f32)], axis=1
            ).astype(bf16)


def head_grads(lay, places, x, dense, vec):
    width = dense[0].shape[1]
    depth = D // lay.peers

    def token(s, q):
        return (token_chunk(lay, s // 4, s % 4, q[1]), 0)

    rows = depth + 16 if lay.direct else D
    whole = lambda s, q: (0, 0)
    spec = pltpu.PrefetchScalarGridSpec(
        num_scalar_prefetch=1,
        grid=(8,),
        in_specs=[
            pl.BlockSpec((256, D), token),
            pl.BlockSpec((256, width), lambda s, q: (jnp.minimum(s, 3), 0)),
            pl.BlockSpec((256, width), lambda s, q: (jnp.maximum(s - 4, 0), 0)),
            pl.BlockSpec(vec.shape, lambda s, q: (0, 0, 0)),
        ],
        out_specs=[pl.BlockSpec((rows, width), whole)] * lay.arrays,
        scratch_shapes=[pltpu.VMEM((D, width), f32)],
    )
    return pl.pallas_call(
        partial(head_grad_kernel, lay),
        grid_spec=spec,
        out_shape=[jax.ShapeDtypeStruct((rows, width), bf16)] * lay.arrays,
        compiler_params=pltpu.CompilerParams(vmem_limit_bytes=VMEM),
        name="head_grads",
        cost_estimate=QUICK,
    )(places, x, *dense, vec)


def finish_heads_kernel(*refs):
    parts, outs = refs[:-7], refs[-7:]
    depth, width = outs[0].shape
    heads = width // HEAD_DIM
    total = parts[0][...].astype(f32)
    for ref in parts[1:]:
        total = total + ref[...].astype(f32)
    grads = total[:depth]
    cut = [slice(h * LANES, h * LANES + HEAD_DIM) for h in range(heads)]
    outs[0][...] = jnp.concatenate([grads[:, at] for at in cut], axis=1)
    cut = [slice(h * LANES + HEAD_DIM, (h + 1) * LANES) for h in range(heads)]
    outs[1][...] = jnp.concatenate([grads[:, at] for at in cut], axis=1)
    outs[2][...] = grads[:, 2 * width : 3 * width]
    vectors = total[depth:, :depth] + total[depth:, LANES : LANES + depth]
    outs[3][...] = vectors[:4]
    outs[4][...] = vectors[4:6]
    outs[5][...] = vectors[6:8]
    outs[6][...] = vectors[8:12]


def finish_heads(parts, depth, width):
    shapes = [(depth, width)] * 3 + [(4, depth), (2, depth), (2, depth), (4, depth)]
    return pl.pallas_call(
        finish_heads_kernel,
        out_shape=[jax.ShapeDtypeStruct(s, f32) for s in shapes],
        name="finish_heads",
        cost_estimate=QUICK,
    )(*parts)


def finish_middle_kernel(grad_ref, inner_ref, outer_ref, output_ref):
    inner_ref[...] = grad_ref[:, :D].astype(f32)
    outer_ref[...] = grad_ref[:, D : 2 * D].astype(f32)
    rest = grad_ref[:, 2 * D :].astype(f32)
    planes = [rest[:, i * LANES : (i + 1) * LANES] for i in range(rest.shape[1] // LANES)]
    folded = [p[:, :HEAD_DIM] + p[:, HEAD_DIM:] for p in planes]
    output_ref[...] = jnp.concatenate(folded, axis=1).T


def finish_middle(grads):
    depth, total = grads.shape
    return pl.pallas_call(
        finish_middle_kernel,
        out_shape=[
            jax.ShapeDtypeStruct((depth, D), f32),
            jax.ShapeDtypeStruct((depth, D), f32),
            jax.ShapeDtypeStruct(((total - 2 * D) // 2, depth), f32),
        ],
        name="finish_middle",
        cost_estimate=QUICK,
    )(grads)


def order_kernel(place_ref, *refs):
    for i in range(4):

        @pl.when(pl.program_id(0) == i)
        def _():
            refs[4][...] = refs[i][...]


def order_quarters(order, quarters):
    rows, width = quarters[0].shape
    cuts = 2
    cut = rows // cuts

    def source(i):
        return lambda s, r, q: (jnp.where(s == i, r, jnp.where(s < i, 0, cuts - 1)), 0)

    spec = pltpu.PrefetchScalarGridSpec(
        num_scalar_prefetch=1,
        grid=(4, cuts),
        in_specs=[pl.BlockSpec((cut, width), source(i)) for i in range(4)],
        out_specs=pl.BlockSpec((cut, width), lambda s, r, q: (q[s] * cuts + r, 0)),
    )
    return pl.pallas_call(
        order_kernel,
        grid_spec=spec,
        out_shape=jax.ShapeDtypeStruct((4 * rows, width), quarters[0].dtype),
        name="order_quarters",
        cost_estimate=QUICK,
    )(order, *quarters)


def over_rows(lay, blocks):
    if not lay.direct:
        return [lax.all_to_all(blocks[0], "dp", split_axis=0, concat_axis=0, tiled=True)]
    out = [blocks[0]]
    for s in range(1, lay.peers):
        out.append(lax.ppermute(blocks[s], "dp", [(i, i ^ s) for i in range(lay.peers)]))
    return out


def in_hbm(rows):
    return pltpu.with_memory_space_constraint(rows, pltpu.HBM)


def after(value, *others):
    return lax.optimization_barrier((value, *others))[0]


def swap(rows, flip):
    return lax.ppermute(rows, "mp", [(i, i ^ flip) for i in range(4)])


def over_heads(blocks):
    return [blocks[0]] + [swap(blocks[t], t) for t in range(1, 4)]


def on_device(
    hidden_in,
    cotangent,
    w_query,
    w_key,
    w_value,
    w_output,
    w_inner,
    w_outer,
    biases,
    gains,
    shifts,
    inner_bias,
    lengths,
    padding,
    cluster_perm,
):
    peers = lax.axis_size("dp")
    tokens = hidden_in.shape[0]
    heads = cluster_perm.shape[0]
    lay = Layout(peers, tokens, heads)
    place = lax.axis_index("mp")
    me = lax.axis_index("dp")
    places = jnp.stack([me, place]).astype(i32)
    hidden_in = in_hbm(hidden_in)
    depth = w_query.shape[0]
    width = heads * HEAD_DIM

    piece, shard, outer_shard = pack_weights(
        w_query, w_key, w_value, w_output, w_inner, w_outer.T,
        biases, gains, shifts, inner_bias.reshape(1, -1),
    )
    inner_w = lax.all_gather(shard, "dp", axis=0, tiled=True)
    outer_w = lax.all_gather(outer_shard, "dp", axis=0, tiled=True)
    if lay.direct:
        weights, bias, params = assemble_weights(lay, places, over_rows(lay, [piece] * peers))
    else:
        weights, bias, params = gather_weights(lay, place, piece)

    weights = in_hbm(weights)
    code = in_hbm(place_tokens(lay, cluster_perm))
    sent = project_rows(lay, places, hidden_in, weights, bias, code, padding.reshape(1, tokens))
    inner_w = after(inner_w, sent[0])
    far_inner = swap(inner_w, 2)
    arrived = over_rows(lay, sent)
    outer_w = after(outer_w, *arrived)
    far_outer = swap(outer_w, 2)
    mixed = over_rows(lay, attend(lay, arrived))
    far_inner, far_outer = after(far_inner, *mixed), after(far_outer, *mixed)
    middle_w = [inner_w, swap(inner_w, 1), far_inner, swap(far_inner, 1)]
    middle_w += [outer_w, swap(outer_w, 1), far_outer, swap(far_outer, 1)]
    att = over_heads(unsort_rows(lay, places, mixed, code))
    saved, att_grad, vec = middle(places, att, hidden_in, cotangent, params, middle_w)
    out_quarter, act, pre_grad, first_low, ffn_grad, branch_grad, grad_h1 = saved
    saved = tuple(in_hbm(a) for a in (act, pre_grad, first_low, ffn_grad, branch_grad))
    att = [in_hbm(a) for a in att]

    got = over_heads(att_grad)
    far = swap(out_quarter, 2)
    summed = weight_grads(places, saved, att)
    grad_h1 = in_hbm(grad_h1)
    summed = lax.psum_scatter(summed, "mp", scatter_dimension=0, tiled=True)
    grads = over_rows(lay, sort_rows(lay, places, got, code))
    grads[0] = after(grads[0], far)
    slot_grads, bias_sums = attend_back(lay, arrived, grads)

    returned = over_rows(lay, slot_grads)
    reduced = lax.psum_scatter(
        after(summed, *returned), "dp", scatter_dimension=0, tiled=True
    )
    hidden_out = order_quarters(
        jnp.stack([place, place ^ 2, place ^ 1, place ^ 3]).astype(i32),
        [out_quarter, after(far, slot_grads[0]), swap(out_quarter, 1), swap(far, 1)],
    )
    head_sums = bias_sums[:, :2].reshape(heads, 2, 2, HEAD_DIM).sum(axis=2)
    head_sums = head_sums.transpose(1, 0, 2).reshape(2, width)
    vec = lax.dynamic_update_slice(vec[:12], head_sums, (0, place * width))
    vec = vec + swap(vec, 1)
    vec = vec + swap(vec, 2)
    vec = jnp.concatenate(
        [vec[:8].reshape(8, peers, depth).transpose(1, 0, 2), vec[8:].reshape(peers, 4, depth)],
        axis=1,
    )
    spread = jnp.pad(vec, ((0, 0), (0, 4), (0, (-depth) % LANES)))
    ready_code = after(code, hidden_out, spread)
    groups = [
        collect(lay, g, places, returned, ready_code, weights, grad_h1) for g in range(2)
    ]
    chips = [
        (mine.astype(f32) + swap(other, 1).astype(f32)).astype(bf16) for other, mine, _ in groups
    ]
    terms = head_grads(lay, places, hidden_in, [dense for _, _, dense in groups], spread)
    if lay.direct:
        ends = finish_heads(over_rows(lay, terms), depth, width)
    else:
        ends = reduce_heads(terms[0], vec, depth, width)
    ready = [
        (after(chip, ends[0]).astype(f32) + swap(chip, 2).astype(f32)).astype(bf16)
        for chip in chips
    ]
    core = place % 2
    grad_hidden = order_quarters(
        jnp.stack([2 * core, 2 * core + 1, 2 - 2 * core, 3 - 2 * core]).astype(i32),
        ready + [swap(part, 1) for part in ready],
    )

    grad_inner, grad_outer, grad_output = finish_middle(reduced)
    return (
        hidden_out,
        grad_hidden,
        ends[0],
        ends[1],
        ends[2],
        grad_output,
        grad_inner,
        grad_outer.T,
        ends[3],
        ends[4],
        ends[5],
        ends[6].reshape(-1),
    )


def gather_weights(lay, place, piece):
    depth = D // lay.peers
    width = lay.heads * HEAD_DIM
    got = lax.all_gather(piece, "dp", axis=0, tiled=False)
    weights = got[:, :depth].reshape(D, -1)
    vectors = got[:, depth : depth + 12, :depth].astype(f32)
    params = vectors[:, :8].transpose(1, 0, 2).reshape(8, D)
    params = jnp.concatenate([params, vectors[:, 8:].reshape(4, D), jnp.zeros((4, D), f32)], axis=0)
    own = lax.dynamic_slice_in_dim(params[:2], place * width, width, 1)
    query = own[0].reshape(lay.heads, HEAD_DIM)
    query = jnp.concatenate([query, jnp.zeros_like(query)], axis=1).reshape(-1)
    row = jnp.concatenate([query, own[1], jnp.zeros(weights.shape[1] - 3 * width, f32)])
    return weights, jnp.broadcast_to(row[None], (8, row.shape[0])), params


def reduce_heads(grads, vec, depth, width):
    total = lax.psum_scatter(grads, "dp", scatter_dimension=0, tiled=True).astype(f32)
    pairs = total[:, : 2 * width].reshape(depth, -1, 2, HEAD_DIM)
    small = lax.psum_scatter(vec, "dp", scatter_dimension=0, tiled=False)
    return (
        pairs[:, :, 0].reshape(depth, width),
        pairs[:, :, 1].reshape(depth, width),
        total[:, 2 * width : 3 * width],
        small[:4],
        small[4:6],
        small[6:8],
        small[8:],
    )


def solution(mesh):
    placed = (
        P("dp", None),
        P("dp", None),
        P("dp", "mp"),
        P("dp", "mp"),
        P("dp", "mp"),
        P("mp", "dp"),
        P("dp", "mp"),
        P("mp", "dp"),
        P(None, "dp"),
        P(None, "dp"),
        P(None, "dp"),
        P("dp"),
        P(),
        P("dp"),
        P("mp", "dp"),
    )
    return jax.shard_map(
        on_device,
        mesh=mesh,
        in_specs=placed,
        out_specs=(
            P("dp", None),
            P("dp", None),
            P("dp", "mp"),
            P("dp", "mp"),
            P("dp", "mp"),
            P("mp", "dp"),
            P("dp", "mp"),
            P("mp", "dp"),
            P(None, "dp"),
            P(None, "dp"),
            P(None, "dp"),
            P("dp"),
        ),
        check_vma=False,
    )
```

time: 566 us -> 510 us (0.901); the launches traced: 564 us -> 502 us
  blocking collectives: 200 us -> 0 us
  waiting for transfers between devices: 102 us -> 218 us
  starting transfers between devices: 15.3 us -> 98 us
  local copies, waits for them, and re-layouts: 56.6 us -> 11.7 us
  other arithmetic: 17.5 us -> 4.59 us
    ppermute x6 -> x65, waiting for transfers between devices: 42.9 us -> 211 us  [the longest x42 164 us: over_rows(): lax.ppermute(blocks[s], 'dp', [(i, i ^ s) for i in range(lay.peers)])]
    all_to_all x4 -> x0, blocking collectives: 125 us -> none  [the longest x3 110 us: over_rows(): return lax.all_to_all(rows, 'dp', split_axis=0, concat_axis=0, tiled=True)]
    ppermute x6 -> x65, starting transfers between devices: 3.66 us -> 97.8 us  [the longest x42 82.2 us: over_rows(): lax.ppermute(blocks[s], 'dp', [(i, i ^ s) for i in range(lay.peers)])]
    all_to_all x3 -> x0, waiting for transfers between devices: 58.8 us -> none  [the longest x2 48.4 us: over_rows(): return lax.all_to_all(rows, 'dp', split_axis=0, concat_axis=0, tiled=True)]
    psum x1 -> x0, blocking collectives: 38.5 us -> none  [on_device(): vec = lax.psum(vec, ('dp', 'mp'))]
    all_gather x1 -> x0, blocking collectives: 36.3 us -> none  [on_device(): lax.all_gather(jnp.concatenate([per_head, tail], axis=0), 'dp', axis=0, t...]
    pallas_call x6 -> x14, Pallas kernels: 86 us -> 114 us  [the longest x2 21.8 us: collect(): pl.pallas_call(partial(collect_kernel, lay, g), grid_spec=spec, out_shape...]
    pallas_call x1, Pallas kernels: 20.9 us -> 2.59 us  [place_tokens(): pl.pallas_call(partial(place_kernel, lay), out_shape=jax.ShapeDtypeStruct...]
  transfers between devices with their start and end apart: 11 -> 69, of which waited for: 6 -> 31; matrix products, arithmetic and copies ran while one was open for 9% -> 1% of each run, Pallas kernels for 22% -> 22%
where the time goes in v2:
time: 510 us; the launch traced here: 502 us
  waiting for transfers between devices  218 us (43%)
  Pallas kernels  155 us (30%)
  starting transfers between devices  98 us (19%)
  between operations  14.6 us (3%)
  local copies, waits for them, and re-layouts  11.7 us (2%)
    ppermute x42, waiting for transfers between devices, over_rows(): lax.ppermute(blocks[s], 'dp', [(i, i ^ s) for i in range(lay.peers)])  164 us
    ppermute x42, starting transfers between devices, over_rows(): lax.ppermute(blocks[s], 'dp', [(i, i ^ s) for i in range(lay.peers)])  82.2 us
    ppermute x23, waiting for transfers between devices, swap(): return lax.ppermute(rows, 'mp', [(i, i ^ flip) for i in range(4)])  47.8 us
    pallas_call x1, Pallas kernels, middle(): pl.pallas_call(middle_kernel, grid_spec=spec, out_shape=[jax.ShapeDtypeSt...  28 us
    pallas_call x2, Pallas kernels, collect(): pl.pallas_call(partial(collect_kernel, lay, g), grid_spec=spec, out_shape...  21.8 us
    pallas_call x1, Pallas kernels, project_rows(): pl.pallas_call(partial(project_kernel, lay, steps), grid_spec=spec, out_s...  17.1 us
    pallas_call x1, Pallas kernels, sort_rows(): pl.pallas_call(partial(sort_kernel, lay), grid_spec=spec, out_shape=lay.s...  16.9 us
    ppermute x23, starting transfers between devices, swap(): return lax.ppermute(rows, 'mp', [(i, i ^ flip) for i in range(4)])  15.6 us
  transfers between devices with their start and end apart: 69, of which 31 were waited for; matrix products, arithmetic and copies ran while one was open for 1% of the time, Pallas kernels for 22%

profile of v2, /device:TPU:0, one launch (start us, length us, event | category | flops | bytes accessed | tf_op | source)
XLA Modules:
  0.0 502.0 jit_solution(12642341004086326537)
XLA Ops:
  31.1 14.6 %collective-permute-done.4.refs_5_ = bf16[112,640]{1,0:T(8,128)(2,1)S(1)} collective-permute-done((bf16[112,640]{1,0:T(8,128)(2,1)}, bf16[112,640]{1,0:T(8,128)(2,1)S(1)}, u32[]{:S(2)}, u32[]{:S(2)}) %collective-permute-start.4) | collective-permute-done | bytes 143392 | tf_op jit(solution)/shard_map/ppermute | solution.py:1072
  49.7 17.1 %project_rows.1 = (bf16[1168,128]{1,0:T(8,128)(2,1)}, bf16[1168,128]{1,0:T(8,128)(2,1)}, bf16[1168,128]{1,0:T(8,128)(2,1)}, bf16[1168,128]{1,0:T(8,128)(2,1)}, b...) custom-call(s32[2]{0:T(128)} %pad_add_fusion.1.place_ref, ...), custom_call_target="tpu_custom_call" | custom-call | flops 1000 | bytes 1000 | tf_op jit(solution)/shard_map/project_rows/pallas_call | solution.py:262
  66.8 6.1 %all-gather.3.cloned.1.call-done.w0 = bf16[768,1152]{1,0:T(8,128)(2,1)} async-done(((bf16[96,1152]{1,0:T(8,128)(2,1)}), bf16[768,1152]{1,0:T(8,128)(2,1)}) %all-gather.3.cloned.1.call-update) | async-done | bytes 1769488 | tf_op jit(solution)/shard_map/all_gather | solution.py:1124
  82.0 33.4 %collective-permute-done.10.refs_4_.refs_12_ = bf16[1168,128]{1,0:T(8,128)(2,1)S(1)} collective-permute-done((bf16[1168,128]{1,0:T(8,128)(2,1)}, bf16[1168,128]{1,0:T(8,128)(2,1)S(1)}, u32[]{:S(2)}, u32[]{:S(2)}) %collective-permute-start.10) | collective-permute-done | bytes 299040 | tf_op jit(solution)/shard_map/ppermute | solution.py:1072
  115.9 5.8 %collective-permute-done.11.refs_5_.refs_13_ = bf16[1168,128]{1,0:T(8,128)(2,1)S(1)} collective-permute-done((bf16[1168,128]{1,0:T(8,128)(2,1)}, bf16[1168,128]{1,0:T(8,128)(2,1)S(1)}, u32[]{:S(2)}, u32[]{:S(2)}) %collective-permute-start.11) | collective-permute-done | bytes 299040 | tf_op jit(solution)/shard_map/ppermute | solution.py:1072
  121.7 9.8 %collective-permute-start.9 = (bf16[1168,128]{1,0:T(8,128)(2,1)}, bf16[1168,128]{1,0:T(8,128)(2,1)S(1)}, u32[]{:S(2)}, u32[]{:S(2)}) collective-permute-start(bf16[1168,128]{1,0:T(8,128)(2,1)} %get-tuple-element.107), channel_id=1, source_target_pairs={{0,12},{4,8},{8,4},{12,0},{16,28},{20,24},{24,20},{28,16},{1,13},{... | collective-permute-start | bytes 897032 | tf_op jit(solution)/shard_map/ppermute | solution.py:1072
  136.0 8.7 %collective-permute-done.9.refs_3_.refs_11_ = bf16[1168,128]{1,0:T(8,128)(2,1)S(1)} collective-permute-done((bf16[1168,128]{1,0:T(8,128)(2,1)}, bf16[1168,128]{1,0:T(8,128)(2,1)S(1)}, u32[]{:S(2)}, u32[]{:S(2)}) %collective-permute-start.9) | collective-permute-done | bytes 299040 | tf_op jit(solution)/shard_map/ppermute | solution.py:1072
  149.2 5.1 %attend.1 = (bf16[384,128]{1,0:T(8,128)(2,1)}, bf16[384,128]{1,0:T(8,128)(2,1)}, bf16[384,128]{1,0:T(8,128)(2,1)}, bf16[384,128]{1,0:T(8,128)(2,1)}, bf16[384,12...) custom-call(bf16[1168,128]{1,0:T(8,128)(2,1)} %get-tuple-element.104.refs_0_.refs, ...), custom_call_target="tpu_custom_call" | custom-call | flops 1000 | bytes 1000 | tf_op jit(solution)/shard_map/attend/pallas_call | solution.py:337
  165.1 7.3 %collective-permute-done.17.refs_4_ = bf16[384,128]{1,0:T(8,128)(2,1)S(1)} collective-permute-done((bf16[384,128]{1,0:T(8,128)(2,1)}, bf16[384,128]{1,0:T(8,128)(2,1)S(1)}, u32[]{:S(2)}, u32[]{:S(2)}) %collective-permute-start.17) | collective-permute-done | bytes 98336 | tf_op jit(solution)/shard_map/ppermute | solution.py:1072
  174.9 4.9 collective-permute-done.20.refs_7_
  180.6 6.6 %unsort_rows.1 = (bf16[256,384]{1,0:T(8,128)(2,1)}, bf16[256,384]{1,0:T(8,128)(2,1)}, bf16[256,384]{1,0:T(8,128)(2,1)}, bf16[256,384]{1,0:T(8,128)(2,1)}) custom-call(s32[2]{0:T(128)} %pad_add_fusion.1.place_ref, bf16[384,128]{1,0:T(8,128)(2,1)} %get-tuple-element.112.refs_0_, bf16[384,128]{1,0:T(8,128)(2,1)} %copy-done.44, bf16[384,128]{1,0:T(8,128)(2,1)} %copy-done.45, ...), custom_call_target="tpu_custom_call" | custom-call | flops 1000 | bytes 1000 | tf_op jit(solution)/shard_map/unsort_rows/pallas_call | solution.py:422
  189.4 6.9 %collective-permute-done.22.att2.refs_2_ = bf16[256,384]{1,0:T(8,128)(2,1)S(1)} collective-permute-done((bf16[256,384]{1,0:T(8,128)(2,1)}, bf16[256,384]{1,0:T(8,128)(2,1)S(1)}, u32[]{:S(2)}, u32[]{:S(2)}) %collective-permute-start.22) | collective-permute-done | bytes 196640 | tf_op jit(solution)/shard_map/ppermute | solution.py:1085
  196.4 7.1 %collective-permute-done.23.att3.refs_3_ = bf16[256,384]{1,0:T(8,128)(2,1)S(1)} collective-permute-done((bf16[256,384]{1,0:T(8,128)(2,1)}, bf16[256,384]{1,0:T(8,128)(2,1)S(1)}, u32[]{:S(2)}, u32[]{:S(2)}) %collective-permute-start.23) | collective-permute-done | bytes 196640 | tf_op jit(solution)/shard_map/ppermute | solution.py:1085
  205.5 28.0 %middle.1 = (bf16[512,768]{1,0:T(8,128)(2,1)}, bf16[512,3072]{1,0:T(8,128)(2,1)}, bf16[512,3072]{1,0:T(8,128)(2,1)}, bf16[512,768]{1,0:T(8,128)(2,1)}, bf16[512,...) custom-call(s32[2]{0:T(128)} %pad_add_fusion.1.place_ref, ...), custom_call_target="tpu_custom_call" | custom-call | flops 1000 | bytes 1000 | tf_op jit(solution)/shard_map/middle/pallas_call | solution.py:780
  233.5 13.4 %weight_grads.1 = bf16[3072,1920]{1,0:T(8,128)(2,1)} custom-call(s32[2]{0:T(128)} %pad_add_fusion.1.place_ref, bf16[512,3072]{1,0:T(8,128)(2,1)} %get-tuple-element.177.act_ref, bf16[512,3072]{1,0:T(8,128)(2,1)} %get-tuple-element.178.pre_ref, bf16[512,768]{1,0:T(8,128)(2,1)} %get-tuple-element.179.low_ref, bf16[512,768]{1,0:T(8,128)(2,1)} %get-tuple-element.180.ffn_ref, ...), custom_call_target="tpu_custom_call" | custom-call | flops 1000 | bytes 1000 | tf_op jit(solution)/shard_map/weight_grads/pallas_call | solution.py:832
  250.3 22.4 %collective-permute-done.32.refs_2_ = bf16[256,384]{1,0:T(8,128)(2,1)S(1)} collective-permute-done((bf16[256,384]{1,0:T(8,128)(2,1)S(1)}, bf16[256,384]{1,0:T(8,128)(2,1)S(1)}, u32[]{:S(2)}, u32[]{:S(2)}) %collective-permute-start.32) | collective-permute-done | bytes 196640 | tf_op jit(solution)/shard_map/ppermute | solution.py:1085
  272.6 5.1 %collective-permute-done.33.refs_3_ = bf16[256,384]{1,0:T(8,128)(2,1)S(1)} collective-permute-done((bf16[256,384]{1,0:T(8,128)(2,1)S(1)}, bf16[256,384]{1,0:T(8,128)(2,1)S(1)}, u32[]{:S(2)}, u32[]{:S(2)}) %collective-permute-start.33) | collective-permute-done | bytes 196640 | tf_op jit(solution)/shard_map/ppermute | solution.py:1085
  278.4 16.9 %sort_rows.1 = (bf16[384,128]{1,0:T(8,128)(2,1)}, bf16[384,128]{1,0:T(8,128)(2,1)}, bf16[384,128]{1,0:T(8,128)(2,1)}, bf16[384,128]{1,0:T(8,128)(2,1)}, bf16[384...) custom-call(s32[2]{0:T(128)} %pad_add_fusion.1.place_ref, ...), custom_call_target="tpu_custom_call" | custom-call | flops 1000 | bytes 1000 | tf_op jit(solution)/shard_map/sort_rows/pallas_call | solution.py:461
  301.4 5.2 %collective-permute-start.40 = (bf16[384,128]{1,0:T(8,128)(2,1)}, bf16[384,128]{1,0:T(8,128)(2,1)S(1)}, u32[]{:S(2)}, u32[]{:S(2)}) collective-permute-start(bf16[384,128]{1,0:T(8,128)(2,1)} %get-tuple-element.144), channel_id=1, source_target_pairs={{0,28},{4,24},{8,20},{12,16},{16,12},{20,8},{24,4},{28,0},{1,29},{... | collective-permute-start | bytes 294920 | tf_op jit(solution)/shard_map/ppermute | solution.py:1072
  306.6 7.0 %collective-permute-done.37.refs_20_ = bf16[384,128]{1,0:T(8,128)(2,1)S(1)} collective-permute-done((bf16[384,128]{1,0:T(8,128)(2,1)}, bf16[384,128]{1,0:T(8,128)(2,1)S(1)}, u32[]{:S(2)}, u32[]{:S(2)}) %collective-permute-start.37) | collective-permute-done | bytes 98336 | tf_op jit(solution)/shard_map/ppermute | solution.py:1072
  316.9 10.4 %attend_back.1 = (bf16[1152,128]{1,0:T(8,128)(2,1)}, bf16[1152,128]{1,0:T(8,128)(2,1)}, bf16[1152,128]{1,0:T(8,128)(2,1)}, bf16[1152,128]{1,0:T(8,128)(2,1)}, bf...) custom-call(bf16[1168,128]{1,0:T(8,128)(2,1)} %get-tuple-element.104, ...), custom_call_target="tpu_custom_call" | custom-call | flops 1000 | bytes 1000 | tf_op jit(solution)/shard_map/attend_back/pallas_call | solution.py:378
  338.4 13.5 %collective-permute-done.44.refs_2_ = bf16[1152,128]{1,0:T(8,128)(2,1)S(1)} collective-permute-done((bf16[1152,128]{1,0:T(8,128)(2,1)}, bf16[1152,128]{1,0:T(8,128)(2,1)S(1)}, u32[]{:S(2)}, u32[]{:S(2)}) %collective-permute-start.44) | collective-permute-done | bytes 294944 | tf_op jit(solution)/shard_map/ppermute | solution.py:1072
  357.0 19.6 %collective-permute-done.47.refs_5_ = bf16[1152,128]{1,0:T(8,128)(2,1)S(1)} collective-permute-done((bf16[1152,128]{1,0:T(8,128)(2,1)}, bf16[1152,128]{1,0:T(8,128)(2,1)S(1)}, u32[]{:S(2)}, u32[]{:S(2)}) %collective-permute-start.47) | collective-permute-done | bytes 294944 | tf_op jit(solution)/shard_map/ppermute | solution.py:1072
  385.3 7.4 %order_quarters.2 = bf16[2048,768]{1,0:T(8,128)(2,1)} custom-call(s32[4]{0:T(128)} %pad_add_fusion.place_ref, bf16[512,768]{1,0:T(8,128)(2,1)} %get-tuple-element.131.refs_0_, bf16[512,768]{1,0:T(8,128)(2,1)} %copy-done.22, bf16[512,768]{1,0:T(8,128)(2,1)} %collective-permute-done.41.refs_2_, bf16[512,768]{1,0:T(8,128)(2,1)} %collective-permute-done.42.refs_3_), custom_call_target="tpu_custom_call" | custom-call | flops 1000 | bytes 1000 | tf_op jit(solution)/shard_map/order_quarters/pallas_call | solution.py:1058
  392.8 10.9 %collect.3 = (bf16[512,768]{1,0:T(8,128)(2,1)}, bf16[512,768]{1,0:T(8,128)(2,1)}, bf16[1024,640]{1,0:T(8,128)(2,1)}) custom-call(s32[2]{0:T(128)} %pad_add_fusion.1.place_ref, bf16[1152,128]{1,0:T(8,128)(2,1)} %get-tuple-element.145.refs_0_, bf16[1152,128]{1,0:T(8,128)(2,1)} %copy-done.11, bf16[1152,128]{1,0:T(8,128)(2,1)} %copy-done.12, ...), custom_call_target="tpu_custom_call" | custom-call | flops 1000 | bytes 1000 | tf_op jit(solution)/shard_map/collect/pallas_call | solution.py:905
  403.7 11.0 %collect.2 = (bf16[512,768]{1,0:T(8,128)(2,1)}, bf16[512,768]{1,0:T(8,128)(2,1)}, bf16[1024,640]{1,0:T(8,128)(2,1)}) custom-call(s32[2]{0:T(128)} %pad_add_fusion.1.place_ref, bf16[1152,128]{1,0:T(8,128)(2,1)} %get-tuple-element.145.refs_0_, bf16[1152,128]{1,0:T(8,128)(2,1)} %copy-done.11, bf16[1152,128]{1,0:T(8,128)(2,1)} %copy-done.12, ...), custom_call_target="tpu_custom_call" | custom-call | flops 1000 | bytes 1000 | tf_op jit(solution)/shard_map/collect/pallas_call | solution.py:905
  418.7 9.3 %head_grads.1 = (bf16[112,640]{1,0:T(8,128)(2,1)}, bf16[112,640]{1,0:T(8,128)(2,1)}, bf16[112,640]{1,0:T(8,128)(2,1)}, bf16[112,640]{1,0:T(8,128)(2,1)}, bf16[11...) custom-call(s32[2]{0:T(128)} %pad_add_fusion.1.place_ref, ...), custom_call_target="tpu_custom_call" | custom-call | flops 1000 | bytes 1000 | tf_op jit(solution)/shard_map/head_grads/pallas_call | solution.py:973
  428.6 11.6 %collective-permute-start.54 = (bf16[112,640]{1,0:T(8,128)(2,1)}, bf16[112,640]{1,0:T(8,128)(2,1)S(1)}, u32[]{:S(2)}, u32[]{:S(2)}) collective-permute-start(bf16[112,640]{1,0:T(8,128)(2,1)} %get-tuple-element.164), channel_id=1, source_target_pairs={{0,8},{4,12},{8,0},{12,4},{16,24},{20,28},{24,16},{28,20},{1,9},{5... | collective-permute-start | bytes 430088 | tf_op jit(solution)/shard_map/ppermute | solution.py:1072
  448.0 8.5 %collective-permute-done.55.refs_3_ = bf16[112,640]{1,0:T(8,128)(2,1)S(1)} collective-permute-done((bf16[112,640]{1,0:T(8,128)(2,1)}, bf16[112,640]{1,0:T(8,128)(2,1)S(1)}, u32[]{:S(2)}, u32[]{:S(2)}) %collective-permute-start.55) | collective-permute-done | bytes 143392 | tf_op jit(solution)/shard_map/ppermute | solution.py:1072
  457.0 9.4 %collective-permute-done.56.refs_4_ = bf16[112,640]{1,0:T(8,128)(2,1)S(1)} collective-permute-done((bf16[112,640]{1,0:T(8,128)(2,1)}, bf16[112,640]{1,0:T(8,128)(2,1)S(1)}, u32[]{:S(2)}, u32[]{:S(2)}) %collective-permute-start.56) | collective-permute-done | bytes 143392 | tf_op jit(solution)/shard_map/ppermute | solution.py:1072
  466.4 11.2 %collective-permute-done.57.refs_5_ = bf16[112,640]{1,0:T(8,128)(2,1)S(1)} collective-permute-done((bf16[112,640]{1,0:T(8,128)(2,1)}, bf16[112,640]{1,0:T(8,128)(2,1)S(1)}, u32[]{:S(2)}, u32[]{:S(2)}) %collective-permute-start.57) | collective-permute-done | bytes 143392 | tf_op jit(solution)/shard_map/ppermute | solution.py:1072
  485.9 7.4 %order_quarters.3 = bf16[2048,768]{1,0:T(8,128)(2,1)} custom-call(s32[4]{0:T(128)} %pad_add_fusion.2.place_ref, bf16[512,768]{1,0:T(8,128)(2,1)} %copy-done.8, bf16[512,768]{1,0:T(8,128)(2,1)} %copy-done.7, bf16[512,768]{1,0:T(8,128)(2,1)} %copy-done.24, bf16[512,768]{1,0:T(8,128)(2,1)} %copy-done.23), custom_call_target="tpu_custom_call" | custom-call | flops 1000 | bytes 1000 | tf_op jit(solution)/shard_map/order_quarters/pallas_call | solution.py:1058
  (276 shorter events, 125.7 us)
Async XLA Ops:
  7.2 65.7 %all-gather.3.cloned.1.call-start = ((), (), s32[]{:S(2)}) async-start(), calls=%async_computation.2 | async-start | bytes 1990656 | tf_op jit(solution)/shard_map/all_gather | solution.py:1124
  10.5 134.2 %all-gather.5.cloned.1.call-start = ((), (), s32[]{:S(2)}) async-start(), calls=%async_computation.3 | async-start | bytes 1327104 | tf_op jit(solution)/shard_map/all_gather | solution.py:1125
  11.3 365.4 %reduce-scatter.3.cloned.1.call-start = ((), (), s32[]{:S(2)}) async-start(), calls=%async_computation.4 | async-start | bytes 14745600 | tf_op jit(solution)/shard_map/reduce_scatter | solution.py:1153
  18.9 26.8 %collective-permute-start.4 = (bf16[112,640]{1,0:T(8,128)(2,1)}, bf16[112,640]{1,0:T(8,128)(2,1)S(1)}, u32[]{:S(2)}, u32[]{:S(2)}) collective-permute-start(bf16[112,640]{1,0:T(8,128)(2,1)} %get-tuple-element.101.refs_0_), channel_id=1, source_target_pairs={{0,20},{4,16},{8,28},{12,24},{16,4},{20,0},{24,12},{28,8},{1,21},{... | collective-permute-start | bytes 430088 | tf_op jit(solution)/shard_map/ppermute | solution.py:1072
  20.2 25.5 %collective-permute-start.5 = (bf16[112,640]{1,0:T(8,128)(2,1)}, bf16[112,640]{1,0:T(8,128)(2,1)S(1)}, u32[]{:S(2)}, u32[]{:S(2)}) collective-permute-start(bf16[112,640]{1,0:T(8,128)(2,1)} %get-tuple-element.101.refs_0_), channel_id=1, source_target_pairs={{0,24},{4,28},{8,16},{12,20},{16,8},{20,12},{24,0},{28,4},{1,25},{... | collective-permute-start | bytes 430088 | tf_op jit(solution)/shard_map/ppermute | solution.py:1072
  27.8 17.9 %collective-permute-start.6 = (bf16[112,640]{1,0:T(8,128)(2,1)}, bf16[112,640]{1,0:T(8,128)(2,1)S(1)}, u32[]{:S(2)}, u32[]{:S(2)}) collective-permute-start(bf16[112,640]{1,0:T(8,128)(2,1)} %get-tuple-element.101.refs_0_), channel_id=1, source_target_pairs={{0,28},{4,24},{8,20},{12,16},{16,12},{20,8},{24,4},{28,0},{1,29},{... | collective-permute-start | bytes 430088 | tf_op jit(solution)/shard_map/ppermute | solution.py:1072
  72.8 107.0 %collective-permute-start.25 = (bf16[768,1152]{1,0:T(8,128)(2,1)}, bf16[768,1152]{1,0:T(8,128)(2,1)}, u32[]{:S(2)}, u32[]{:S(2)}) collective-permute-start(bf16[768,1152]{1,0:T(8,128)(2,1)} %all-gather.3.cloned.1.call-done.w0), channel_id=1, source_target_pairs={{0,2},{1,3},{2,0},{3,1},{4,6},{5,7},{6,4},{7,5},{8,10},{9,11},{10,... | collective-permute-start | bytes 5308424 | tf_op jit(solution)/shard_map/ppermute | solution.py:1085
  74.4 41.1 %collective-permute-start.10 = (bf16[1168,128]{1,0:T(8,128)(2,1)}, bf16[1168,128]{1,0:T(8,128)(2,1)S(1)}, u32[]{:S(2)}, u32[]{:S(2)}) collective-permute-start(bf16[1168,128]{1,0:T(8,128)(2,1)} %get-tuple-element.108), channel_id=1, source_target_pairs={{0,16},{4,20},{8,24},{12,28},{16,0},{20,4},{24,8},{28,12},{1,17},{... | collective-permute-start | bytes 897032 | tf_op jit(solution)/shard_map/ppermute | solution.py:1072
  76.7 45.0 %collective-permute-start.11 = (bf16[1168,128]{1,0:T(8,128)(2,1)}, bf16[1168,128]{1,0:T(8,128)(2,1)S(1)}, u32[]{:S(2)}, u32[]{:S(2)}) collective-permute-start(bf16[1168,128]{1,0:T(8,128)(2,1)} %get-tuple-element.109), channel_id=1, source_target_pairs={{0,20},{4,16},{8,28},{12,24},{16,4},{20,0},{24,12},{28,8},{1,21},{... | collective-permute-start | bytes 897032 | tf_op jit(solution)/shard_map/ppermute | solution.py:1072
  77.2 44.5 %collective-permute-start.12 = (bf16[1168,128]{1,0:T(8,128)(2,1)}, bf16[1168,128]{1,0:T(8,128)(2,1)S(1)}, u32[]{:S(2)}, u32[]{:S(2)}) collective-permute-start(bf16[1168,128]{1,0:T(8,128)(2,1)} %get-tuple-element.110), channel_id=1, source_target_pairs={{0,24},{4,28},{8,16},{12,20},{16,8},{20,12},{24,0},{28,4},{1,25},{... | collective-permute-start | bytes 897032 | tf_op jit(solution)/shard_map/ppermute | solution.py:1072
  79.5 52.0 %collective-permute-start.13 = (bf16[1168,128]{1,0:T(8,128)(2,1)}, bf16[1168,128]{1,0:T(8,128)(2,1)S(1)}, u32[]{:S(2)}, u32[]{:S(2)}) collective-permute-start(bf16[1168,128]{1,0:T(8,128)(2,1)} %get-tuple-element.111), channel_id=1, source_target_pairs={{0,28},{4,24},{8,20},{12,16},{16,12},{20,8},{24,4},{28,0},{1,29},{... | collective-permute-start | bytes 897032 | tf_op jit(solution)/shard_map/ppermute | solution.py:1072
  121.7 23.0 %collective-permute-start.9 = (bf16[1168,128]{1,0:T(8,128)(2,1)}, bf16[1168,128]{1,0:T(8,128)(2,1)S(1)}, u32[]{:S(2)}, u32[]{:S(2)}) collective-permute-start(bf16[1168,128]{1,0:T(8,128)(2,1)} %get-tuple-element.107), channel_id=1, source_target_pairs={{0,12},{4,8},{8,4},{12,0},{16,28},{20,24},{24,20},{28,16},{1,13},{... | collective-permute-start | bytes 897032 | tf_op jit(solution)/shard_map/ppermute | solution.py:1072
  144.7 35.7 %collective-permute-start.28 = (bf16[768,768]{1,0:T(8,128)(2,1)}, bf16[768,768]{1,0:T(8,128)(2,1)}, u32[]{:S(2)}, u32[]{:S(2)}) collective-permute-start(bf16[768,768]{1,0:T(8,128)(2,1)} %all-gather.5.cloned.1.call-done.v0), channel_id=1, source_target_pairs={{0,2},{1,3},{2,0},{3,1},{4,6},{5,7},{6,4},{7,5},{8,10},{9,11},{10,... | collective-permute-start | bytes 3538952 | tf_op jit(solution)/shard_map/ppermute | solution.py:1085
  174.9 28.6 %collective-permute-start.24 = (bf16[768,1152]{1,0:T(8,128)(2,1)}, bf16[768,1152]{1,0:T(8,128)(2,1)S(1)}, u32[]{:S(2)}, u32[]{:S(2)}) collective-permute-start(bf16[768,1152]{1,0:T(8,128)(2,1)} %all-gather.3.cloned.1.call-done.w0), channel_id=1, source_target_pairs={{0,1},{1,0},{2,3},{3,2},{4,5},{5,4},{6,7},{7,6},{8,9},{9,8},{10,11... | collective-permute-start | bytes 5308424 | tf_op jit(solution)/shard_map/ppermute | solution.py:1085
  179.9 23.7 %collective-permute-start.26 = (bf16[768,1152]{1,0:T(8,128)(2,1)}, bf16[768,1152]{1,0:T(8,128)(2,1)S(1)}, u32[]{:S(2)}, u32[]{:S(2)}) collective-permute-start(bf16[768,1152]{1,0:T(8,128)(2,1)} %collective-permute-done.25.w2), channel_id=1, source_target_pairs={{0,1},{1,0},{2,3},{3,2},{4,5},{5,4},{6,7},{7,6},{8,9},{9,8},{10,11... | collective-permute-start | bytes 5308424 | tf_op jit(solution)/shard_map/ppermute | solution.py:1085
  179.9 23.6 %collective-permute-start.27 = (bf16[768,768]{1,0:T(8,128)(2,1)}, bf16[768,768]{1,0:T(8,128)(2,1)}, u32[]{:S(2)}, u32[]{:S(2)}) collective-permute-start(bf16[768,768]{1,0:T(8,128)(2,1)} %all-gather.5.cloned.1.call-done.v0), channel_id=1, source_target_pairs={{0,1},{1,0},{2,3},{3,2},{4,5},{5,4},{6,7},{7,6},{8,9},{9,8},{10,11... | collective-permute-start | bytes 3538952 | tf_op jit(solution)/shard_map/ppermute | solution.py:1085
  180.5 23.0 %collective-permute-start.29 = (bf16[768,768]{1,0:T(8,128)(2,1)}, bf16[768,768]{1,0:T(8,128)(2,1)}, u32[]{:S(2)}, u32[]{:S(2)}) collective-permute-start(bf16[768,768]{1,0:T(8,128)(2,1)} %collective-permute-done.28.v2), channel_id=1, source_target_pairs={{0,1},{1,0},{2,3},{3,2},{4,5},{5,4},{6,7},{7,6},{8,9},{9,8},{10,11... | collective-permute-start | bytes 3538952 | tf_op jit(solution)/shard_map/ppermute | solution.py:1085
  246.9 246.4 %reduce-scatter.5.cloned.1.call-start = ((), (), s32[]{:S(2)}) async-start(), calls=%async_computation.5 | async-start | bytes 3317760 | tf_op jit(solution)/shard_map/reduce_scatter | solution.py:1159
  248.0 53.4 %collective-permute-start.30 = (bf16[512,768]{1,0:T(8,128)(2,1)S(1)}, bf16[512,768]{1,0:T(8,128)(2,1)S(1)}, u32[]{:S(2)}, u32[]{:S(2)}) collective-permute-start(bf16[512,768]{1,0:T(8,128)(2,1)S(1)} %copy-done.21), channel_id=1, source_target_pairs={{0,2},{1,3},{2,0},{3,1},{4,6},{5,7},{6,4},{7,5},{8,10},{9,11},{10,... | collective-permute-start | bytes 2359304 | tf_op jit(solution)/shard_map/ppermute | solution.py:1085
  248.4 24.2 %collective-permute-start.32 = (bf16[256,384]{1,0:T(8,128)(2,1)S(1)}, bf16[256,384]{1,0:T(8,128)(2,1)S(1)}, u32[]{:S(2)}, u32[]{:S(2)}) collective-permute-start(bf16[256,384]{1,0:T(8,128)(2,1)S(1)} %copy-done.61), channel_id=1, source_target_pairs={{0,2},{1,3},{2,0},{3,1},{4,6},{5,7},{6,4},{7,5},{8,10},{9,11},{10,... | collective-permute-start | bytes 589832 | tf_op jit(solution)/shard_map/ppermute | solution.py:1085
  250.1 27.7 %collective-permute-start.33 = (bf16[256,384]{1,0:T(8,128)(2,1)S(1)}, bf16[256,384]{1,0:T(8,128)(2,1)S(1)}, u32[]{:S(2)}, u32[]{:S(2)}) collective-permute-start(bf16[256,384]{1,0:T(8,128)(2,1)S(1)} %copy-done.60), channel_id=1, source_target_pairs={{0,3},{1,2},{2,1},{3,0},{4,7},{5,6},{6,5},{7,4},{8,11},{9,10},{10,... | collective-permute-start | bytes 589832 | tf_op jit(solution)/shard_map/ppermute | solution.py:1085
  328.9 22.9 %collective-permute-start.44 = (bf16[1152,128]{1,0:T(8,128)(2,1)}, bf16[1152,128]{1,0:T(8,128)(2,1)S(1)}, u32[]{:S(2)}, u32[]{:S(2)}) collective-permute-start(bf16[1152,128]{1,0:T(8,128)(2,1)} %get-tuple-element.148), channel_id=1, source_target_pairs={{0,8},{4,12},{8,0},{12,4},{16,24},{20,28},{24,16},{28,20},{1,9},{5... | collective-permute-start | bytes 884744 | tf_op jit(solution)/shard_map/ppermute | solution.py:1072
  333.1 23.9 %collective-permute-start.45 = (bf16[1152,128]{1,0:T(8,128)(2,1)}, bf16[1152,128]{1,0:T(8,128)(2,1)S(1)}, u32[]{:S(2)}, u32[]{:S(2)}) collective-permute-start(bf16[1152,128]{1,0:T(8,128)(2,1)} %get-tuple-element.149), channel_id=1, source_target_pairs={{0,12},{4,8},{8,4},{12,0},{16,28},{20,24},{24,20},{28,16},{1,13},{... | collective-permute-start | bytes 884744 | tf_op jit(solution)/shard_map/ppermute | solution.py:1072
  333.1 23.9 %collective-permute-start.46 = (bf16[1152,128]{1,0:T(8,128)(2,1)}, bf16[1152,128]{1,0:T(8,128)(2,1)S(1)}, u32[]{:S(2)}, u32[]{:S(2)}) collective-permute-start(bf16[1152,128]{1,0:T(8,128)(2,1)} %get-tuple-element.150), channel_id=1, source_target_pairs={{0,16},{4,20},{8,24},{12,28},{16,0},{20,4},{24,8},{28,12},{1,17},{... | collective-permute-start | bytes 884744 | tf_op jit(solution)/shard_map/ppermute | solution.py:1072
  334.9 41.7 %collective-permute-start.47 = (bf16[1152,128]{1,0:T(8,128)(2,1)}, bf16[1152,128]{1,0:T(8,128)(2,1)S(1)}, u32[]{:S(2)}, u32[]{:S(2)}) collective-permute-start(bf16[1152,128]{1,0:T(8,128)(2,1)} %get-tuple-element.151), channel_id=1, source_target_pairs={{0,20},{4,16},{8,28},{12,24},{16,4},{20,0},{24,12},{28,8},{1,21},{... | collective-permute-start | bytes 884744 | tf_op jit(solution)/shard_map/ppermute | solution.py:1072
  336.9 39.7 %collective-permute-start.48 = (bf16[1152,128]{1,0:T(8,128)(2,1)}, bf16[1152,128]{1,0:T(8,128)(2,1)S(1)}, u32[]{:S(2)}, u32[]{:S(2)}) collective-permute-start(bf16[1152,128]{1,0:T(8,128)(2,1)} %get-tuple-element.152), channel_id=1, source_target_pairs={{0,24},{4,28},{8,16},{12,20},{16,8},{20,12},{24,0},{28,4},{1,25},{... | collective-permute-start | bytes 884744 | tf_op jit(solution)/shard_map/ppermute | solution.py:1072
  351.8 24.8 %collective-permute-start.49 = (bf16[1152,128]{1,0:T(8,128)(2,1)}, bf16[1152,128]{1,0:T(8,128)(2,1)S(1)}, u32[]{:S(2)}, u32[]{:S(2)}) collective-permute-start(bf16[1152,128]{1,0:T(8,128)(2,1)} %get-tuple-element.153), channel_id=1, source_target_pairs={{0,28},{4,24},{8,20},{12,16},{16,12},{20,8},{24,4},{28,0},{1,29},{... | collective-permute-start | bytes 884744 | tf_op jit(solution)/shard_map/ppermute | solution.py:1072
  415.4 65.2 %collective-permute-start.62 = (bf16[512,768]{1,0:T(8,128)(2,1)S(1)}, bf16[512,768]{1,0:T(8,128)(2,1)S(1)}, u32[]{:S(2)}, u32[]{:S(2)}) collective-permute-start(bf16[512,768]{1,0:T(8,128)(2,1)S(1)} %add_convert_fusion.1), channel_id=1, source_target_pairs={{0,2},{1,3},{2,0},{3,1},{4,6},{5,7},{6,4},{7,5},{8,10},{9,11},{10,... | collective-permute-start | bytes 2359304 | tf_op jit(solution)/shard_map/ppermute | solution.py:1085
  417.5 63.4 %collective-permute-start.60 = (bf16[512,768]{1,0:T(8,128)(2,1)S(1)}, bf16[512,768]{1,0:T(8,128)(2,1)}, u32[]{:S(2)}, u32[]{:S(2)}) collective-permute-start(bf16[512,768]{1,0:T(8,128)(2,1)S(1)} %add_convert_fusion.3), channel_id=1, source_target_pairs={{0,2},{1,3},{2,0},{3,1},{4,6},{5,7},{6,4},{7,5},{8,10},{9,11},{10,... | collective-permute-start | bytes 2359304 | tf_op jit(solution)/shard_map/ppermute | solution.py:1085
  441.2 25.2 %collective-permute-start.56 = (bf16[112,640]{1,0:T(8,128)(2,1)}, bf16[112,640]{1,0:T(8,128)(2,1)S(1)}, u32[]{:S(2)}, u32[]{:S(2)}) collective-permute-start(bf16[112,640]{1,0:T(8,128)(2,1)} %get-tuple-element.166), channel_id=1, source_target_pairs={{0,16},{4,20},{8,24},{12,28},{16,0},{20,4},{24,8},{28,12},{1,17},{... | collective-permute-start | bytes 430088 | tf_op jit(solution)/shard_map/ppermute | solution.py:1072
  446.1 31.5 %collective-permute-start.57 = (bf16[112,640]{1,0:T(8,128)(2,1)}, bf16[112,640]{1,0:T(8,128)(2,1)S(1)}, u32[]{:S(2)}, u32[]{:S(2)}) collective-permute-start(bf16[112,640]{1,0:T(8,128)(2,1)} %get-tuple-element.167), channel_id=1, source_target_pairs={{0,20},{4,16},{8,28},{12,24},{16,4},{20,0},{24,12},{28,8},{1,21},{... | collective-permute-start | bytes 430088 | tf_op jit(solution)/shard_map/ppermute | solution.py:1072
  456.6 21.0 %collective-permute-start.58 = (bf16[112,640]{1,0:T(8,128)(2,1)}, bf16[112,640]{1,0:T(8,128)(2,1)S(1)}, u32[]{:S(2)}, u32[]{:S(2)}) collective-permute-start(bf16[112,640]{1,0:T(8,128)(2,1)} %get-tuple-element.168), channel_id=1, source_target_pairs={{0,24},{4,28},{8,16},{12,20},{16,8},{20,12},{24,0},{28,4},{1,25},{... | collective-permute-start | bytes 430088 | tf_op jit(solution)/shard_map/ppermute | solution.py:1072
  (100 other events, 1091.9 us)
Sparse Core Ops, SparseCore 0:
  10.8 62.0 all-gather.2
  75.6 67.0 all-gather.4
  247.0 93.4 reduce-scatter.2
  376.8 100.5 reduce-scatter.4
